TPU v7x, 256 devices: a whole 4x4x8 slice. The times are simulated.
256 devices in a mesh: src: 32 (over z, y_lo, core), tgt: 8 (over y_hi, x).
Axes of the slice: x: 4, y: 4 (y_hi: 2, y_lo: 2; y = y_hi * 2 + y_lo), z: 8, core: 2. Of those that a mesh axis runs over, the one named last changes fastest.
Arguments:
- inputs: bfloat16 [512, 2, 1024, 512], P(('src', 'tgt')), may hold values from -6 to 6
- leaf_maps: bfloat16 [512, 2, 256, 1024], P(('src', 'tgt')), may hold values from -0.125 to 0.125
- transfer_blocks: bfloat16 [4, 512, 2, 2, 256, 256], P(None, ('src', 'tgt')), may hold values from -0.1875 to 0.1875
Outputs:
- butterfly_out: bfloat16 [512, 2, 256, 512], P(('src', 'tgt'))
All inputs are finite; a program needn't handle non-finite values.
Results may differ from a plain program's by a relative error of at most 0.012.
Values may be sent and summed in bfloat16 or wider, within the bound.
No kernel may reach another device: no remote copies, remote signals or barrier semaphores. Data moves between devices by JAX's collectives and lax.ppermute only.
A program may use at most 64 MiB of HBM per device.

v0:
```python
import jax
import jax.numpy as jnp
from jax import lax
from jax.sharding import PartitionSpec as P


def partner_2(block, axis, apart):
    count = lax.axis_size(axis)
    route = []
    for low in range(count):
        high = low | 1 << apart
        if high != low and high < count:
            route += [(low, high), (high, low)]
    return lax.ppermute(block, axis, route)


def batched(left_side, right_side):
    return jnp.einsum("nij,njr->nir", left_side, right_side, preferred_element_type=jnp.float32)


def complex_product(blocks, vectors):
    real_part = batched(blocks[:, 0], vectors[:, 0]) - batched(blocks[:, 1], vectors[:, 1])
    imag_part = batched(blocks[:, 0], vectors[:, 1]) + batched(blocks[:, 1], vectors[:, 0])
    return jnp.stack([real_part, imag_part], axis=1)


def remote_term(coeffs, other_blocks, axis_src, bit_place):
    partial_term = complex_product(other_blocks, coeffs).astype(jnp.bfloat16)
    if axis_src:
        arrived = partner_2(partial_term, "src", bit_place)
    else:
        arrived = partner_2(partial_term, "tgt", bit_place)
    return arrived.astype(jnp.float32)


def butterfly_level(coeffs, blocks, axis_src, bit_place):
    device_index = lax.axis_index("src") if axis_src else lax.axis_index("tgt")
    own_bit = device_index // 2**bit_place % 2
    kept_blocks = lax.dynamic_index_in_dim(blocks, own_bit, axis=1, keepdims=False)
    other_blocks = lax.dynamic_index_in_dim(blocks, 1 - own_bit, axis=1, keepdims=False)
    local_term = complex_product(kept_blocks, coeffs)
    return (local_term + remote_term(coeffs, other_blocks, axis_src, bit_place)).astype(
        jnp.bfloat16
    )


def local(inputs, leaf_maps, transfer_blocks):
    coeffs = complex_product(leaf_maps, inputs).astype(jnp.bfloat16)
    first_blocks = transfer_blocks[0]
    halves = []
    for target_bit in range(2):
        other_bit = 1 - target_bit
        own_term = complex_product(
            first_blocks[target_bit : target_bit + 1, target_bit],
            coeffs[target_bit : target_bit + 1],
        )[0]
        partner = complex_product(
            first_blocks[other_bit : other_bit + 1, target_bit], coeffs[other_bit : other_bit + 1]
        )[0].astype(jnp.bfloat16)
        halves.append(own_term + partner.astype(jnp.float32))
    coeffs = jnp.stack(halves, axis=0).astype(jnp.bfloat16)
    src_bits = lax.axis_size("src").bit_length() - 1
    tgt_bits = lax.axis_size("tgt").bit_length() - 1
    coeffs = butterfly_level(coeffs, transfer_blocks[1], True, src_bits - 1)
    coeffs = butterfly_level(coeffs, transfer_blocks[2], True, src_bits - 2)
    return butterfly_level(coeffs, transfer_blocks[3], False, tgt_bits - 1)


def solution(mesh):
    placed = (
        P(("src", "tgt"), None, None, None),
        P(("src", "tgt"), None, None, None),
        P(None, ("src", "tgt"), None, None, None, None),
    )
    return jax.shard_map(
        local,
        mesh=mesh,
        in_specs=placed,
        out_specs=P(("src", "tgt"), None, None, None),
        check_vma=False,
    )
```

profile of v0, /device:TPU:1, one launch (start us, length us, event | category | flops | bytes accessed | tf_op | source)
XLA Modules:
  0.0 155.3 jit_solution(10111678524155202634)
XLA Ops:
  0.0 2.8 %fusion.3 = f32[2,256,512]{2,1,0:T(8,128)S(1)} fusion(bf16[2,2,1024,512]{3,2,1,0:T(8,128)(2,1)} %param.3, bf16[2,2,256,1024]{3,2,1,0:T(8,128)(2,1)} %param.4), kind=kOutput, calls=%fused_computation.6 | convolution fusion | flops 536870912 | bytes 4194304 | tf_op jit(solution)/shard_map/nij,njr->nir/dot_general | solution.py:18
  2.8 0.4 copy-done.17
  3.1 2.1 %fusion.5 = f32[2,256,512]{2,1,0:T(8,128)S(1)} fusion(bf16[2,2,1024,512]{3,2,1,0:T(8,128)(2,1)S(1)} %copy-done.17, bf16[2,2,256,1024]{3,2,1,0:T(8,128)(2,1)} %param.4), kind=kOutput, calls=%fused_computation.8 | convolution fusion | flops 536870912 | bytes 4194304 | tf_op jit(solution)/shard_map/nij,njr->nir/dot_general | solution.py:18
  5.2 0.7 fusion.33
  6.0 0.7 fusion.36
  6.7 1.5 copy-done
  8.1 1.4 fusion.90
  9.6 1.1 fusion.89
  10.7 1.1 fusion.87
  11.7 1.1 fusion.84
  12.8 1.1 fusion.82
  13.9 1.1 fusion.88
  14.9 1.1 fusion.86
  16.0 1.1 fusion.85
  17.1 1.1 fusion.83
  18.2 0.9 constant_dynamic-slice_fusion.2
  19.1 0.4 copy-done.11
  22.6 0.3 fusion.81
  23.0 0.3 fusion.80
  23.3 0.3 fusion.44
  23.7 0.3 fusion.43
  24.0 1.1 pad_maximum_fusion
  25.1 7.7 %collective-permute-start = (bf16[2,2,256,512]{3,2,0,1:T(8,128)(2,1)}, bf16[2,2,256,512]{3,2,0,1:T(8,128)(2,1)}, u32[]{:S(2)}, u32[]{:S(2)}) collective-permute-start(bf16[2,2,256,512]{3,2,0,1:T(8,128)(2,1)} %pad_maximum_fusion), channel_id=1, source_target_pairs={{0,128},{128,0},{8,136},{136,8},{16,144},{144,16},{24,152},{152,24... | collective-permute-start | bytes 3145736 | tf_op jit(solution)/shard_map/ppermute | solution.py:14
  33.1 0.8 copy-done.16
  33.9 0.3 fusion.79
  34.3 0.3 fusion.26
  34.6 0.3 fusion.78
  34.9 0.3 fusion.25
  35.3 26.2 %collective-permute-done = bf16[2,2,256,512]{3,2,0,1:T(8,128)(2,1)} collective-permute-done((bf16[2,2,256,512]{3,2,0,1:T(8,128)(2,1)}, bf16[2,2,256,512]{3,2,0,1:T(8,128)(2,1)}, u32[]{:S(2)}, u32[]{:S(2)}) %collective-permute-start) | collective-permute-done | bytes 1048608 | tf_op jit(solution)/shard_map/ppermute | solution.py:14
  61.4 1.6 %fusion = bf16[2,2,256,512]{3,2,0,1:T(8,128)(2,1)S(1)} fusion(f32[2,1,256,512]{3,2,0,1:T(8,128)S(1)} %fusion.25, f32[2,1,256,512]{3,2,0,1:T(8,128)S(1)} %fusion.26, bf16[2,2,256,512]{3,2,0,1:T(8,128)(2,1)} %collective-permute-done), kind=kLoop, calls=%fused_computation.1 | loop fusion | flops 2097152 | bytes 4194304 | tf_op jit(solution)/shard_map/convert_element_type | solution.py:42
  63.3 0.3 fusion.70
  63.6 0.3 fusion.42
  63.9 0.3 fusion.41
  64.4 18.7 %collective-permute-start.1 = (bf16[2,2,256,512]{3,2,0,1:T(8,128)(2,1)S(1)}, bf16[2,2,256,512]{3,2,0,1:T(8,128)(2,1)S(1)}, u32[]{:S(2)}, u32[]{:S(2)}) collective-permute-start(bf16[2,2,256,512]{3,2,0,1:T(8,128)(2,1)S(1)} %pad_maximum_fusion.1), channel_id=1, source_target_pairs={{0,64},{64,0},{8,72},{72,8},{16,80},{80,16},{24,88},{88,24},{32,96... | collective-permute-start | bytes 3145736 | tf_op jit(solution)/shard_map/ppermute | solution.py:14
  83.5 0.3 fusion.23
  84.1 0.3 fusion.24
  84.4 43.4 %collective-permute-done.1 = bf16[2,2,256,512]{3,2,0,1:T(8,128)(2,1)S(1)} collective-permute-done((bf16[2,2,256,512]{3,2,0,1:T(8,128)(2,1)S(1)}, bf16[2,2,256,512]{3,2,0,1:T(8,128)(2,1)S(1)}, u32[]{:S(2)}, u32[]{:S(2)}) %collective-permute-start.1) | collective-permute-done | bytes 1048608 | tf_op jit(solution)/shard_map/ppermute | solution.py:14
  127.8 0.4 fusion.1
  128.2 0.3 fusion.76
  128.5 0.3 fusion.74
  128.8 0.3 fusion.40
  129.1 0.3 fusion.39
  129.5 3.0 %collective-permute-start.2 = (bf16[2,2,256,512]{3,2,0,1:T(8,128)(2,1)S(1)}, bf16[2,2,256,512]{3,2,0,1:T(8,128)(2,1)S(1)}, u32[]{:S(2)}, u32[]{:S(2)}) collective-permute-start(bf16[2,2,256,512]{3,2,0,1:T(8,128)(2,1)S(1)} %pad_maximum_fusion.2), channel_id=1, source_target_pairs={{0,4},{4,0},{1,5},{5,1},{2,6},{6,2},{3,7},{7,3},{8,12},{12,8},{9,1... | collective-permute-start | bytes 3145736 | tf_op jit(solution)/shard_map/ppermute | solution.py:14
  132.8 0.3 fusion.21
  133.4 0.3 fusion.22
  133.7 20.2 %collective-permute-done.2 = bf16[2,2,256,512]{3,2,0,1:T(8,128)(2,1)S(1)} collective-permute-done((bf16[2,2,256,512]{3,2,0,1:T(8,128)(2,1)S(1)}, bf16[2,2,256,512]{3,2,0,1:T(8,128)(2,1)S(1)}, u32[]{:S(2)}, u32[]{:S(2)}) %collective-permute-start.2) | collective-permute-done | bytes 1048608 | tf_op jit(solution)/shard_map/ppermute | solution.py:14
  153.9 0.4 fusion.2
  154.2 1.0 copy.22
  (59 shorter events, 5.2 us)
Async XLA Ops:
  0.0 3.1 %copy-start.17 = (bf16[2,2,1024,512]{3,2,1,0:T(8,128)(2,1)S(1)}, bf16[2,2,1024,512]{3,2,1,0:T(8,128)(2,1)}, u32[]{:S(2)}) copy-start(bf16[2,2,1024,512]{3,2,1,0:T(8,128)(2,1)} %param.3) | copy-start | bytes 12582916
  3.1 2.1 %copy-start.18 = (bf16[2,2,256,1024]{3,2,1,0:T(8,128)(2,1)S(1)}, bf16[2,2,256,1024]{3,2,1,0:T(8,128)(2,1)}, u32[]{:S(2)}) copy-start(bf16[2,2,256,1024]{3,2,1,0:T(8,128)(2,1)} %param.4) | copy-start | bytes 6291460
  5.9 2.2 %copy-start = (bf16[4,2,2,2,256,256]{5,4,3,2,1,0:T(8,128)(2,1)S(1)}, bf16[4,2,2,2,256,256]{5,4,3,2,1,0:T(8,128)(2,1)}, u32[]{:S(2)}) copy-start(bf16[4,2,2,2,256,256]{5,4,3,2,1,0:T(8,128)(2,1)} %param.5) | copy-start | bytes 12582916
  9.6 5.4 %copy-start.2 = (bf16[1,2,256,256]{3,2,1,0:T(8,128)(2,1)}, bf16[1,2,256,256]{3,2,1,0:T(8,128)(2,1)S(1)}, u32[]{:S(2)}) copy-start(bf16[1,2,256,256]{3,2,1,0:T(8,128)(2,1)S(1)} %get-tuple-element.17) | copy-start | bytes 786436
  9.6 5.3 %copy-start.6 = (bf16[1,2,256,256]{3,2,1,0:T(8,128)(2,1)}, bf16[1,2,256,256]{3,2,1,0:T(8,128)(2,1)S(1)}, u32[]{:S(2)}) copy-start(bf16[1,2,256,256]{3,2,1,0:T(8,128)(2,1)S(1)} %get-tuple-element.19) | copy-start | bytes 786436
  9.6 7.5 %copy-start.4 = (bf16[1,2,256,256]{3,2,1,0:T(8,128)(2,1)}, bf16[1,2,256,256]{3,2,1,0:T(8,128)(2,1)S(1)}, u32[]{:S(2)}) copy-start(bf16[1,2,256,256]{3,2,1,0:T(8,128)(2,1)S(1)} %get-tuple-element.20) | copy-start | bytes 786436
  18.2 0.9 copy-start.3
  18.2 1.3 copy-start.11
  18.2 1.6 %copy-start.10 = (f32[512,256]{1,0:T(8,128)S(1)}, f32[512,256]{1,0:T(8,128)}, u32[]{:S(2)}) copy-start(f32[512,256]{1,0:T(8,128)} %fusion.87) | copy-start | bytes 1572868
  19.0 1.1 copy-start.9
  19.0 1.4 copy-start.8
  19.5 1.3 copy-start.7
  19.5 1.3 copy-start.15
  20.2 1.1 copy-start.14
  20.5 1.1 copy-start.5
  20.5 1.2 copy-start.13
  20.8 1.2 copy-start.12
  23.6 9.2 %copy-start.1 = (bf16[1,2,2,2,256,256]{5,4,3,2,1,0:T(8,128)(2,1)S(1)}, bf16[1,2,2,2,256,256]{5,4,3,2,1,0:T(8,128)(2,1)}, u32[]{:S(2)}) copy-start(bf16[1,2,2,2,256,256]{5,4,3,2,1,0:T(8,128)(2,1)} %get-tuple-element.6) | copy-start | bytes 3145732
  25.1 36.3 %collective-permute-start = (bf16[2,2,256,512]{3,2,0,1:T(8,128)(2,1)}, bf16[2,2,256,512]{3,2,0,1:T(8,128)(2,1)}, u32[]{:S(2)}, u32[]{:S(2)}) collective-permute-start(bf16[2,2,256,512]{3,2,0,1:T(8,128)(2,1)} %pad_maximum_fusion), channel_id=1, source_target_pairs={{0,128},{128,0},{8,136},{136,8},{16,144},{144,16},{24,152},{152,24... | collective-permute-start | bytes 3145736 | tf_op jit(solution)/shard_map/ppermute | solution.py:14
  32.8 1.0 copy-start.16
  64.4 63.5 %collective-permute-start.1 = (bf16[2,2,256,512]{3,2,0,1:T(8,128)(2,1)S(1)}, bf16[2,2,256,512]{3,2,0,1:T(8,128)(2,1)S(1)}, u32[]{:S(2)}, u32[]{:S(2)}) collective-permute-start(bf16[2,2,256,512]{3,2,0,1:T(8,128)(2,1)S(1)} %pad_maximum_fusion.1), channel_id=1, source_target_pairs={{0,64},{64,0},{8,72},{72,8},{16,80},{80,16},{24,88},{88,24},{32,96... | collective-permute-start | bytes 3145736 | tf_op jit(solution)/shard_map/ppermute | solution.py:14
  129.5 24.4 %collective-permute-start.2 = (bf16[2,2,256,512]{3,2,0,1:T(8,128)(2,1)S(1)}, bf16[2,2,256,512]{3,2,0,1:T(8,128)(2,1)S(1)}, u32[]{:S(2)}, u32[]{:S(2)}) collective-permute-start(bf16[2,2,256,512]{3,2,0,1:T(8,128)(2,1)S(1)} %pad_maximum_fusion.2), channel_id=1, source_target_pairs={{0,4},{4,0},{1,5},{5,1},{2,6},{6,2},{3,7},{7,3},{8,12},{12,8},{9,1... | collective-permute-start | bytes 3145736 | tf_op jit(solution)/shard_map/ppermute | solution.py:14
where the time goes:
time: 157 us; the launch traced here: 155 us
  waiting for transfers between devices  89.7 us (57%)
  starting transfers between devices  29.4 us (19%)
  matrix products  24.4 us (16%)
  local copies, waits for them, and re-layouts  7.3 us (5%)
  other arithmetic  4 us (3%)
    ppermute x3, waiting for transfers between devices, partner_2(): return lax.ppermute(block, axis, route)  89.7 us
    ppermute x3, starting transfers between devices, partner_2(): return lax.ppermute(block, axis, route)  29.4 us
    dot_general x44, matrix products, batched(): jnp.einsum('nij,njr->nir', left_side, right_side, preferred_element_type=...  24.4 us
    unnamed x38, local copies, waits for them, and re-layouts  3.59 us
  transfers between devices with their start and end apart: 3, of which 3 were waited for; matrix products, arithmetic and copies ran while one was open for 3% of the time, Pallas kernels for 0%

commit v1 on v0

v1 whole, which is shorter than its diff:
```python
import functools

import jax
import jax.numpy as jnp
from jax import lax
from jax.experimental import pallas as pl
from jax.experimental.pallas import tpu as pltpu
from jax.sharding import PartitionSpec as P

CHUNKS = 4
VMEM_LIMIT = 40 * 1024 * 1024


def partner_2(block, axis, apart):
    count = lax.axis_size(axis)
    route = []
    for low in range(count):
        high = low | 1 << apart
        if high != low and high < count:
            route += [(low, high), (high, low)]
    return lax.ppermute(block, axis, route)


def own_bit(axis, place):
    return lax.rem(lax.div(lax.axis_index(axis), 2**place), 2)


def product(blocks, vectors):
    stacked = vectors.reshape(2 * vectors.shape[1], vectors.shape[2])
    real_rows = jnp.concatenate([blocks[0], -blocks[1]], axis=1)
    imag_rows = jnp.concatenate([blocks[1], blocks[0]], axis=1)
    real_part = jnp.dot(real_rows, stacked, preferred_element_type=jnp.float32)
    imag_part = jnp.dot(imag_rows, stacked, preferred_element_type=jnp.float32)
    return jnp.stack([real_part, imag_part])


def first_kernel(chunk, width, place, x_hbm, l_hbm, t_hbm, a_ref, p_ref, x, l, t0, t1, sems):
    other = 1 - own_bit(*place)
    columns = pl.ds(chunk * width, width)
    moves = []
    for b in range(2):
        moves.append(pltpu.make_async_copy(l_hbm.at[b], l.at[b], sems.at[b]))
        moves.append(pltpu.make_async_copy(x_hbm.at[b, :, :, columns], x.at[b], sems.at[2 + b]))
    moves.append(pltpu.make_async_copy(t_hbm.at[0], t0, sems.at[4]))
    moves.append(pltpu.make_async_copy(t_hbm.at[1, :, other], t1, sems.at[5]))
    for move in moves:
        move.start()
    coeffs = []
    for b in range(2):
        moves[2 * b].wait()
        moves[2 * b + 1].wait()
        coeffs.append(product(l[b], x[b]).astype(jnp.bfloat16))
    moves[4].wait()
    after = []
    for b in range(2):
        own_term = product(t0[b, b], coeffs[b])
        partner = product(t0[1 - b, b], coeffs[1 - b]).astype(jnp.bfloat16)
        after.append((own_term + partner.astype(jnp.float32)).astype(jnp.bfloat16))
        a_ref[b] = after[b]
    moves[5].wait()
    for b in range(2):
        p_ref[b] = product(t1[b], after[b]).astype(jnp.bfloat16)


def middle_kernel(level, place, next_place, a_ref, in_ref, t_hbm, a_out, p_out, kept, send, sems):
    own = own_bit(*place)
    other = 1 - own_bit(*next_place)
    moves = [
        pltpu.make_async_copy(t_hbm.at[level, :, own], kept, sems.at[0]),
        pltpu.make_async_copy(t_hbm.at[level + 1, :, other], send, sems.at[1]),
    ]
    for move in moves:
        move.start()
    moves[0].wait()
    after = []
    for b in range(2):
        own_term = product(kept[b], a_ref[b])
        after.append((own_term + in_ref[b].astype(jnp.float32)).astype(jnp.bfloat16))
        a_out[b] = after[b]
    moves[1].wait()
    for b in range(2):
        p_out[b] = product(send[b], after[b]).astype(jnp.bfloat16)


def last_kernel(level, chunk, width, place, a_ref, in_ref, t_hbm, *refs):
    out_hbm, kept, out, sems = refs[-4:]
    own = own_bit(*place)
    move = pltpu.make_async_copy(t_hbm.at[level, :, own], kept, sems.at[0])
    move.start()
    move.wait()
    for b in range(2):
        own_term = product(kept[b], a_ref[b])
        out[b] = (own_term + in_ref[b].astype(jnp.float32)).astype(jnp.bfloat16)
    store = pltpu.make_async_copy(out, out_hbm.at[:, :, :, pl.ds(chunk * width, width)], sems.at[1])
    store.start()
    store.wait()


def local(inputs, leaf_maps, transfer_blocks):
    nodes, _, rank, rows = leaf_maps.shape
    columns = inputs.shape[3]
    width = columns // CHUNKS
    src_bits = lax.axis_size("src").bit_length() - 1
    tgt_bits = lax.axis_size("tgt").bit_length() - 1
    places = [None, ("src", src_bits - 1), ("src", src_bits - 2), ("tgt", tgt_bits - 1)]

    part = jax.ShapeDtypeStruct((nodes, 2, rank, width), jnp.bfloat16)
    anywhere = pl.BlockSpec(memory_space=pltpu.HBM)
    here = pl.BlockSpec(memory_space=pltpu.VMEM)
    params = pltpu.CompilerParams(vmem_limit_bytes=VMEM_LIMIT)
    one_product = 8 * rank * rank * width * nodes
    half_level = pltpu.VMEM((nodes, 2, rank, rank), jnp.bfloat16)

    def first(chunk):
        return pl.pallas_call(
            functools.partial(first_kernel, chunk, width, places[1]),
            out_shape=(part, part),
            in_specs=[anywhere] * 3,
            out_specs=(here, here),
            scratch_shapes=[
                pltpu.VMEM((nodes, 2, rows, width), jnp.bfloat16),
                pltpu.VMEM((nodes, 2, rank, rows), jnp.bfloat16),
                pltpu.VMEM((nodes, 2, 2, rank, rank), jnp.bfloat16),
                half_level,
                pltpu.SemaphoreType.DMA((6,)),
            ],
            compiler_params=params,
            cost_estimate=pl.CostEstimate(
                flops=one_product * (rows // rank + 3), bytes_accessed=5 * 2**20, transcendentals=0
            ),
            name="first",
        )(inputs, leaf_maps, transfer_blocks)

    def middle(level, held, arrived):
        return pl.pallas_call(
            functools.partial(middle_kernel, level, places[level], places[level + 1]),
            out_shape=(part, part),
            in_specs=[here, here, anywhere],
            out_specs=(here, here),
            scratch_shapes=[half_level, half_level, pltpu.SemaphoreType.DMA((2,))],
            compiler_params=params,
            cost_estimate=pl.CostEstimate(
                flops=one_product * 2, bytes_accessed=2 * 2**20, transcendentals=0
            ),
            name="middle",
        )(held, arrived, transfer_blocks)

    def last(level, chunk, held, arrived, result):
        operands = (held, arrived, transfer_blocks)
        aliases = {}
        if result is not None:
            operands += (result,)
            aliases = {3: 0}
        return pl.pallas_call(
            functools.partial(last_kernel, level, chunk, width, places[level]),
            out_shape=jax.ShapeDtypeStruct((nodes, 2, rank, columns), jnp.bfloat16),
            in_specs=[here, here, anywhere] + [anywhere] * len(aliases),
            out_specs=anywhere,
            scratch_shapes=[
                half_level,
                pltpu.VMEM((nodes, 2, rank, width), jnp.bfloat16),
                pltpu.SemaphoreType.DMA((2,)),
            ],
            input_output_aliases=aliases,
            compiler_params=params,
            cost_estimate=pl.CostEstimate(
                flops=one_product, bytes_accessed=2**20, transcendentals=0
            ),
            name="last",
        )(*operands)

    held = [None] * CHUNKS
    flying = [None] * CHUNKS
    for chunk in range(CHUNKS):
        held[chunk], term = first(chunk)
        flying[chunk] = partner_2(term, *places[1])
    for level in (1, 2):
        for chunk in range(CHUNKS):
            held[chunk], term = middle(level, held[chunk], flying[chunk])
            flying[chunk] = partner_2(term, *places[level + 1])
    result = None
    for chunk in range(CHUNKS):
        result = last(3, chunk, held[chunk], flying[chunk], result)
    return result


def solution(mesh):
    placed = (
        P(("src", "tgt"), None, None, None),
        P(("src", "tgt"), None, None, None),
        P(None, ("src", "tgt"), None, None, None, None),
    )
    return jax.shard_map(
        local,
        mesh=mesh,
        in_specs=placed,
        out_specs=P(("src", "tgt"), None, None, None),
        check_vma=False,
    )
```

time: 157 us -> 120 us (0.76); the launches traced: 155 us -> 120 us
  waiting for transfers between devices: 89.7 us -> 55.1 us
  matrix products: 24.4 us -> 0 us
  Pallas kernels: 0 us -> 24.3 us
  starting transfers between devices: 29.4 us -> 34.5 us
  other arithmetic: 4 us -> 0 us
    ppermute x3 -> x12, waiting for transfers between devices: 89.7 us -> 55.1 us  [partner_2(): return lax.ppermute(block, axis, route)]
    dot_general x44 -> x0, matrix products: 24.4 us -> none  [batched(): jnp.einsum('nij,njr->nir', left_side, right_side, preferred_element_type=...]
    pallas_call x0 -> x16, Pallas kernels: none -> 24.3 us  [the longest x4 12 us: first(): pl.pallas_call(functools.partial(first_kernel, chunk, width, places[1]),...]
    ppermute x3 -> x12, starting transfers between devices: 29.4 us -> 34.5 us  [partner_2(): return lax.ppermute(block, axis, route)]
    unnamed x38 -> x6, local copies, waits for them, and re-layouts: 3.59 us -> 5.97 us
    convert_element_type x3 -> x0, other arithmetic: 2.31 us -> none  [butterfly_level(): (local_term + remote_term(coeffs, other_blocks, axis_src, bit_place)).ast...]
    another operation x4 -> x0, other arithmetic: 1.6 us -> none  [the longest x3 1.3 us: complex_product(): return jnp.stack([real_part, imag_part], axis=1)]
  transfers between devices with their start and end apart: 3 -> 12, of which waited for: 3 -> 8; matrix products, arithmetic and copies ran while one was open for 3% -> 0% of each run, Pallas kernels for 0% -> 17%
where the time goes in v1:
time: 120 us
  waiting for transfers between devices  55.1 us (46%)
  starting transfers between devices  34.5 us (29%)
  Pallas kernels  24.3 us (20%)
  local copies, waits for them, and re-layouts  5.97 us (5%)
    ppermute x12, waiting for transfers between devices, partner_2(): return lax.ppermute(block, axis, route)  55.1 us
    ppermute x12, starting transfers between devices, partner_2(): return lax.ppermute(block, axis, route)  34.5 us
    pallas_call x4, Pallas kernels, first(): pl.pallas_call(functools.partial(first_kernel, chunk, width, places[1]),...  12 us
    pallas_call x8, Pallas kernels, middle(): pl.pallas_call(functools.partial(middle_kernel, level, places[level], pla...  7.51 us
    unnamed x6, local copies, waits for them, and re-layouts  5.97 us
    pallas_call x4, Pallas kernels, last(): pl.pallas_call(functools.partial(last_kernel, level, chunk, width, places...  4.76 us
  transfers between devices with their start and end apart: 12, of which 8 were waited for; matrix products, arithmetic and copies ran while one was open for 0% of the time, Pallas kernels for 17%

profile of v1, /device:TPU:1, one launch (start us, length us, event | category | flops | bytes accessed | tf_op | source)
XLA Modules:
  0.0 120.2 jit_solution(9322338536952587922)
XLA Ops:
  0.0 0.0 copy-start
  0.0 2.2 %copy-done = bf16[4,2,2,2,256,256]{5,4,3,2,1,0:T(8,128)(2,1)S(1)} copy-done((bf16[4,2,2,2,256,256]{5,4,3,2,1,0:T(8,128)(2,1)S(1)}, bf16[4,2,2,2,256,256]{5,4,3,2,1,0:T(8,128)(2,1)}, u32[]{:S(2)}) %copy-start) | copy-done | bytes 4194328
  2.2 0.0 copy-start.1
  2.2 2.2 %copy-done.1 = bf16[2,2,1024,512]{3,2,1,0:T(8,128)(2,1)S(1)} copy-done((bf16[2,2,1024,512]{3,2,1,0:T(8,128)(2,1)S(1)}, bf16[2,2,1024,512]{3,2,1,0:T(8,128)(2,1)}, u32[]{:S(2)}) %copy-start.1) | copy-done | bytes 4194328
  4.4 0.0 copy-start.2
  4.4 1.6 %copy-done.2 = bf16[2,2,256,1024]{3,2,1,0:T(8,128)(2,1)S(1)} copy-done((bf16[2,2,256,1024]{3,2,1,0:T(8,128)(2,1)S(1)}, bf16[2,2,256,1024]{3,2,1,0:T(8,128)(2,1)}, u32[]{:S(2)}) %copy-start.2) | copy-done | bytes 2097176
  6.0 3.0 %first.7 = (bf16[2,2,256,128]{3,2,1,0:T(8,128)(2,1)S(1)}, bf16[2,2,256,128]{3,2,1,0:T(8,128)(2,1)S(1)}) custom-call(bf16[2,2,1024,512]{3,2,1,0:T(8,128)(2,1)S(1)} %copy-done.1, bf16[2,2,256,1024]{3,2,1,0:T(8,128)(2,1)S(1)} %copy-done.2, bf16[4,2,2,2,256,256]{5,4,3,2,1,0:T(8,128)(2,1)S(1)} %copy-done), custom_call_target="tpu_custom_call" | custom-call | flops 939524096 | bytes 5242880 | tf_op jit(solution)/shard_map/first/pallas_call | solution.py:115
  9.0 7.8 %collective-permute-start.9 = (bf16[2,2,256,128]{3,2,1,0:T(8,128)(2,1)S(1)}, bf16[2,2,256,128]{3,2,1,0:T(8,128)(2,1)S(1)}, u32[]{:S(2)}, u32[]{:S(2)}) collective-permute-start(bf16[2,2,256,128]{3,2,1,0:T(8,128)(2,1)S(1)} %get-tuple-element.48), channel_id=1, source_target_pairs={{0,128},{128,0},{8,136},{136,8},{16,144},{144,16},{24,152},{152,24... | collective-permute-start | bytes 786440 | tf_op jit(solution)/shard_map/ppermute | solution.py:21
  16.8 3.0 %first.6 = (bf16[2,2,256,128]{3,2,1,0:T(8,128)(2,1)S(1)}, bf16[2,2,256,128]{3,2,1,0:T(8,128)(2,1)S(1)}) custom-call(bf16[2,2,1024,512]{3,2,1,0:T(8,128)(2,1)S(1)} %copy-done.1, bf16[2,2,256,1024]{3,2,1,0:T(8,128)(2,1)S(1)} %copy-done.2, bf16[4,2,2,2,256,256]{5,4,3,2,1,0:T(8,128)(2,1)S(1)} %copy-done), custom_call_target="tpu_custom_call" | custom-call | flops 939524096 | bytes 5242880 | tf_op jit(solution)/shard_map/first/pallas_call | solution.py:115
  19.8 0.1 collective-permute-start.6
  19.9 3.0 %first.5 = (bf16[2,2,256,128]{3,2,1,0:T(8,128)(2,1)S(1)}, bf16[2,2,256,128]{3,2,1,0:T(8,128)(2,1)S(1)}) custom-call(bf16[2,2,1024,512]{3,2,1,0:T(8,128)(2,1)S(1)} %copy-done.1, bf16[2,2,256,1024]{3,2,1,0:T(8,128)(2,1)S(1)} %copy-done.2, bf16[4,2,2,2,256,256]{5,4,3,2,1,0:T(8,128)(2,1)S(1)} %copy-done), custom_call_target="tpu_custom_call" | custom-call | flops 939524096 | bytes 5242880 | tf_op jit(solution)/shard_map/first/pallas_call | solution.py:115
  22.9 5.6 %collective-permute-start.3 = (bf16[2,2,256,128]{3,2,1,0:T(8,128)(2,1)S(1)}, bf16[2,2,256,128]{3,2,1,0:T(8,128)(2,1)S(1)}, u32[]{:S(2)}, u32[]{:S(2)}) collective-permute-start(bf16[2,2,256,128]{3,2,1,0:T(8,128)(2,1)S(1)} %get-tuple-element.36), channel_id=1, source_target_pairs={{0,128},{128,0},{8,136},{136,8},{16,144},{144,16},{24,152},{152,24... | collective-permute-start | bytes 786440 | tf_op jit(solution)/shard_map/ppermute | solution.py:21
  28.6 3.0 %first.4 = (bf16[2,2,256,128]{3,2,1,0:T(8,128)(2,1)S(1)}, bf16[2,2,256,128]{3,2,1,0:T(8,128)(2,1)S(1)}) custom-call(bf16[2,2,1024,512]{3,2,1,0:T(8,128)(2,1)S(1)} %copy-done.1, bf16[2,2,256,1024]{3,2,1,0:T(8,128)(2,1)S(1)} %copy-done.2, bf16[4,2,2,2,256,256]{5,4,3,2,1,0:T(8,128)(2,1)S(1)} %copy-done), custom_call_target="tpu_custom_call" | custom-call | flops 939524096 | bytes 5242880 | tf_op jit(solution)/shard_map/first/pallas_call | solution.py:115
  31.6 0.1 collective-permute-start
  31.7 0.0 collective-permute-done.9.in_ref
  31.7 0.9 middle.14
  32.6 1.5 %collective-permute-start.10 = (bf16[2,2,256,128]{3,2,1,0:T(8,128)(2,1)S(1)}, bf16[2,2,256,128]{3,2,1,0:T(8,128)(2,1)S(1)}, u32[]{:S(2)}, u32[]{:S(2)}) collective-permute-start(bf16[2,2,256,128]{3,2,1,0:T(8,128)(2,1)S(1)} %get-tuple-element.50), channel_id=1, source_target_pairs={{0,64},{64,0},{8,72},{72,8},{16,80},{80,16},{24,88},{88,24},{32,96... | collective-permute-start | bytes 786440 | tf_op jit(solution)/shard_map/ppermute | solution.py:21
  34.1 1.0 collective-permute-done.6.in_ref
  35.1 0.9 middle.12
  36.1 6.2 %collective-permute-start.7 = (bf16[2,2,256,128]{3,2,1,0:T(8,128)(2,1)S(1)}, bf16[2,2,256,128]{3,2,1,0:T(8,128)(2,1)S(1)}, u32[]{:S(2)}, u32[]{:S(2)}) collective-permute-start(bf16[2,2,256,128]{3,2,1,0:T(8,128)(2,1)S(1)} %get-tuple-element.44), channel_id=1, source_target_pairs={{0,64},{64,0},{8,72},{72,8},{16,80},{80,16},{24,88},{88,24},{32,96... | collective-permute-start | bytes 786440 | tf_op jit(solution)/shard_map/ppermute | solution.py:21
  42.2 8.0 %collective-permute-done.3.in_ref = bf16[2,2,256,128]{3,2,1,0:T(8,128)(2,1)S(1)} collective-permute-done((bf16[2,2,256,128]{3,2,1,0:T(8,128)(2,1)S(1)}, bf16[2,2,256,128]{3,2,1,0:T(8,128)(2,1)S(1)}, u32[]{:S(2)}, u32[]{:S(2)}) %collective-permute-start.3) | collective-permute-done | bytes 262176 | tf_op jit(solution)/shard_map/ppermute | solution.py:21
  50.3 0.9 middle.10
  51.2 0.9 collective-permute-start.4
  52.1 11.9 %collective-permute-done.in_ref = bf16[2,2,256,128]{3,2,1,0:T(8,128)(2,1)S(1)} collective-permute-done((bf16[2,2,256,128]{3,2,1,0:T(8,128)(2,1)S(1)}, bf16[2,2,256,128]{3,2,1,0:T(8,128)(2,1)S(1)}, u32[]{:S(2)}, u32[]{:S(2)}) %collective-permute-start) | collective-permute-done | bytes 262176 | tf_op jit(solution)/shard_map/ppermute | solution.py:21
  64.0 0.9 middle.8
  64.9 0.1 collective-permute-start.1
  65.0 26.7 %collective-permute-done.10.in_ref = bf16[2,2,256,128]{3,2,1,0:T(8,128)(2,1)S(1)} collective-permute-done((bf16[2,2,256,128]{3,2,1,0:T(8,128)(2,1)S(1)}, bf16[2,2,256,128]{3,2,1,0:T(8,128)(2,1)S(1)}, u32[]{:S(2)}, u32[]{:S(2)}) %collective-permute-start.10) | collective-permute-done | bytes 262176 | tf_op jit(solution)/shard_map/ppermute | solution.py:21
  91.7 0.9 middle.15
  92.6 3.0 %collective-permute-start.11 = (bf16[2,2,256,128]{3,2,1,0:T(8,128)(2,1)S(1)}, bf16[2,2,256,128]{3,2,1,0:T(8,128)(2,1)S(1)}, u32[]{:S(2)}, u32[]{:S(2)}) collective-permute-start(bf16[2,2,256,128]{3,2,1,0:T(8,128)(2,1)S(1)} %get-tuple-element.52), channel_id=1, source_target_pairs={{0,4},{4,0},{1,5},{5,1},{2,6},{6,2},{3,7},{7,3},{8,12},{12,8},{9,1... | collective-permute-start | bytes 786440 | tf_op jit(solution)/shard_map/ppermute | solution.py:21
  95.6 1.7 %collective-permute-done.7.in_ref = bf16[2,2,256,128]{3,2,1,0:T(8,128)(2,1)S(1)} collective-permute-done((bf16[2,2,256,128]{3,2,1,0:T(8,128)(2,1)S(1)}, bf16[2,2,256,128]{3,2,1,0:T(8,128)(2,1)S(1)}, u32[]{:S(2)}, u32[]{:S(2)}) %collective-permute-start.7) | collective-permute-done | bytes 262176 | tf_op jit(solution)/shard_map/ppermute | solution.py:21
  97.3 0.9 middle.13
  98.2 3.0 %collective-permute-start.8 = (bf16[2,2,256,128]{3,2,1,0:T(8,128)(2,1)S(1)}, bf16[2,2,256,128]{3,2,1,0:T(8,128)(2,1)S(1)}, u32[]{:S(2)}, u32[]{:S(2)}) collective-permute-start(bf16[2,2,256,128]{3,2,1,0:T(8,128)(2,1)S(1)} %get-tuple-element.46), channel_id=1, source_target_pairs={{0,4},{4,0},{1,5},{5,1},{2,6},{6,2},{3,7},{7,3},{8,12},{12,8},{9,1... | collective-permute-start | bytes 786440 | tf_op jit(solution)/shard_map/ppermute | solution.py:21
  101.2 1.7 %collective-permute-done.4.in_ref = bf16[2,2,256,128]{3,2,1,0:T(8,128)(2,1)S(1)} collective-permute-done((bf16[2,2,256,128]{3,2,1,0:T(8,128)(2,1)S(1)}, bf16[2,2,256,128]{3,2,1,0:T(8,128)(2,1)S(1)}, u32[]{:S(2)}, u32[]{:S(2)}) %collective-permute-start.4) | collective-permute-done | bytes 262176 | tf_op jit(solution)/shard_map/ppermute | solution.py:21
  102.9 0.9 middle.11
  103.8 3.2 %collective-permute-start.5 = (bf16[2,2,256,128]{3,2,1,0:T(8,128)(2,1)S(1)}, bf16[2,2,256,128]{3,2,1,0:T(8,128)(2,1)S(1)}, u32[]{:S(2)}, u32[]{:S(2)}) collective-permute-start(bf16[2,2,256,128]{3,2,1,0:T(8,128)(2,1)S(1)} %get-tuple-element.40), channel_id=1, source_target_pairs={{0,4},{4,0},{1,5},{5,1},{2,6},{6,2},{3,7},{7,3},{8,12},{12,8},{9,1... | collective-permute-start | bytes 786440 | tf_op jit(solution)/shard_map/ppermute | solution.py:21
  107.1 1.5 %collective-permute-done.1.in_ref = bf16[2,2,256,128]{3,2,1,0:T(8,128)(2,1)S(1)} collective-permute-done((bf16[2,2,256,128]{3,2,1,0:T(8,128)(2,1)S(1)}, bf16[2,2,256,128]{3,2,1,0:T(8,128)(2,1)S(1)}, u32[]{:S(2)}, u32[]{:S(2)}) %collective-permute-start.1) | collective-permute-done | bytes 262176 | tf_op jit(solution)/shard_map/ppermute | solution.py:21
  108.5 0.9 middle.9
  109.5 3.0 %collective-permute-start.2 = (bf16[2,2,256,128]{3,2,1,0:T(8,128)(2,1)S(1)}, bf16[2,2,256,128]{3,2,1,0:T(8,128)(2,1)S(1)}, u32[]{:S(2)}, u32[]{:S(2)}) collective-permute-start(bf16[2,2,256,128]{3,2,1,0:T(8,128)(2,1)S(1)} %get-tuple-element.34), channel_id=1, source_target_pairs={{0,4},{4,0},{1,5},{5,1},{2,6},{6,2},{3,7},{7,3},{8,12},{12,8},{9,1... | collective-permute-start | bytes 786440 | tf_op jit(solution)/shard_map/ppermute | solution.py:21
  112.5 0.0 collective-permute-done.11.in_ref
  112.5 1.2 last.4.refs_0_
  113.7 0.0 collective-permute-done.8.in_ref
  113.7 1.2 last.5.refs_0_
  114.9 0.0 collective-permute-done.5.in_ref
  114.9 1.2 last.6.refs_0_
  116.1 2.8 %collective-permute-done.2.in_ref = bf16[2,2,256,128]{3,2,1,0:T(8,128)(2,1)S(1)} collective-permute-done((bf16[2,2,256,128]{3,2,1,0:T(8,128)(2,1)S(1)}, bf16[2,2,256,128]{3,2,1,0:T(8,128)(2,1)S(1)}, u32[]{:S(2)}, u32[]{:S(2)}) %collective-permute-start.2) | collective-permute-done | bytes 262176 | tf_op jit(solution)/shard_map/ppermute | solution.py:21
  118.9 1.2 last.7
Async XLA Ops:
  0.0 2.2 %copy-start = (bf16[4,2,2,2,256,256]{5,4,3,2,1,0:T(8,128)(2,1)S(1)}, bf16[4,2,2,2,256,256]{5,4,3,2,1,0:T(8,128)(2,1)}, u32[]{:S(2)}) copy-start(bf16[4,2,2,2,256,256]{5,4,3,2,1,0:T(8,128)(2,1)} %t_hbm.31) | copy-start | bytes 12582916
  2.2 2.2 %copy-start.1 = (bf16[2,2,1024,512]{3,2,1,0:T(8,128)(2,1)S(1)}, bf16[2,2,1024,512]{3,2,1,0:T(8,128)(2,1)}, u32[]{:S(2)}) copy-start(bf16[2,2,1024,512]{3,2,1,0:T(8,128)(2,1)} %x_hbm.7) | copy-start | bytes 12582916
  4.4 1.6 %copy-start.2 = (bf16[2,2,256,1024]{3,2,1,0:T(8,128)(2,1)S(1)}, bf16[2,2,256,1024]{3,2,1,0:T(8,128)(2,1)}, u32[]{:S(2)}) copy-start(bf16[2,2,256,1024]{3,2,1,0:T(8,128)(2,1)} %l_hbm.7) | copy-start | bytes 6291460
  9.0 22.7 %collective-permute-start.9 = (bf16[2,2,256,128]{3,2,1,0:T(8,128)(2,1)S(1)}, bf16[2,2,256,128]{3,2,1,0:T(8,128)(2,1)S(1)}, u32[]{:S(2)}, u32[]{:S(2)}) collective-permute-start(bf16[2,2,256,128]{3,2,1,0:T(8,128)(2,1)S(1)} %get-tuple-element.48), channel_id=1, source_target_pairs={{0,128},{128,0},{8,136},{136,8},{16,144},{144,16},{24,152},{152,24... | collective-permute-start | bytes 786440 | tf_op jit(solution)/shard_map/ppermute | solution.py:21
  19.8 15.3 %collective-permute-start.6 = (bf16[2,2,256,128]{3,2,1,0:T(8,128)(2,1)S(1)}, bf16[2,2,256,128]{3,2,1,0:T(8,128)(2,1)S(1)}, u32[]{:S(2)}, u32[]{:S(2)}) collective-permute-start(bf16[2,2,256,128]{3,2,1,0:T(8,128)(2,1)S(1)} %get-tuple-element.42), channel_id=1, source_target_pairs={{0,128},{128,0},{8,136},{136,8},{16,144},{144,16},{24,152},{152,24... | collective-permute-start | bytes 786440 | tf_op jit(solution)/shard_map/ppermute | solution.py:21
  22.9 27.3 %collective-permute-start.3 = (bf16[2,2,256,128]{3,2,1,0:T(8,128)(2,1)S(1)}, bf16[2,2,256,128]{3,2,1,0:T(8,128)(2,1)S(1)}, u32[]{:S(2)}, u32[]{:S(2)}) collective-permute-start(bf16[2,2,256,128]{3,2,1,0:T(8,128)(2,1)S(1)} %get-tuple-element.36), channel_id=1, source_target_pairs={{0,128},{128,0},{8,136},{136,8},{16,144},{144,16},{24,152},{152,24... | collective-permute-start | bytes 786440 | tf_op jit(solution)/shard_map/ppermute | solution.py:21
  31.6 32.4 %collective-permute-start = (bf16[2,2,256,128]{3,2,1,0:T(8,128)(2,1)S(1)}, bf16[2,2,256,128]{3,2,1,0:T(8,128)(2,1)S(1)}, u32[]{:S(2)}, u32[]{:S(2)}) collective-permute-start(bf16[2,2,256,128]{3,2,1,0:T(8,128)(2,1)S(1)} %get-tuple-element.30), channel_id=1, source_target_pairs={{0,128},{128,0},{8,136},{136,8},{16,144},{144,16},{24,152},{152,24... | collective-permute-start | bytes 786440 | tf_op jit(solution)/shard_map/ppermute | solution.py:21
  32.6 59.0 %collective-permute-start.10 = (bf16[2,2,256,128]{3,2,1,0:T(8,128)(2,1)S(1)}, bf16[2,2,256,128]{3,2,1,0:T(8,128)(2,1)S(1)}, u32[]{:S(2)}, u32[]{:S(2)}) collective-permute-start(bf16[2,2,256,128]{3,2,1,0:T(8,128)(2,1)S(1)} %get-tuple-element.50), channel_id=1, source_target_pairs={{0,64},{64,0},{8,72},{72,8},{16,80},{80,16},{24,88},{88,24},{32,96... | collective-permute-start | bytes 786440 | tf_op jit(solution)/shard_map/ppermute | solution.py:21
  36.1 61.2 %collective-permute-start.7 = (bf16[2,2,256,128]{3,2,1,0:T(8,128)(2,1)S(1)}, bf16[2,2,256,128]{3,2,1,0:T(8,128)(2,1)S(1)}, u32[]{:S(2)}, u32[]{:S(2)}) collective-permute-start(bf16[2,2,256,128]{3,2,1,0:T(8,128)(2,1)S(1)} %get-tuple-element.44), channel_id=1, source_target_pairs={{0,64},{64,0},{8,72},{72,8},{16,80},{80,16},{24,88},{88,24},{32,96... | collective-permute-start | bytes 786440 | tf_op jit(solution)/shard_map/ppermute | solution.py:21
  51.2 51.7 %collective-permute-start.4 = (bf16[2,2,256,128]{3,2,1,0:T(8,128)(2,1)S(1)}, bf16[2,2,256,128]{3,2,1,0:T(8,128)(2,1)S(1)}, u32[]{:S(2)}, u32[]{:S(2)}) collective-permute-start(bf16[2,2,256,128]{3,2,1,0:T(8,128)(2,1)S(1)} %get-tuple-element.38), channel_id=1, source_target_pairs={{0,64},{64,0},{8,72},{72,8},{16,80},{80,16},{24,88},{88,24},{32,96... | collective-permute-start | bytes 786440 | tf_op jit(solution)/shard_map/ppermute | solution.py:21
  64.9 43.6 %collective-permute-start.1 = (bf16[2,2,256,128]{3,2,1,0:T(8,128)(2,1)S(1)}, bf16[2,2,256,128]{3,2,1,0:T(8,128)(2,1)S(1)}, u32[]{:S(2)}, u32[]{:S(2)}) collective-permute-start(bf16[2,2,256,128]{3,2,1,0:T(8,128)(2,1)S(1)} %get-tuple-element.32), channel_id=1, source_target_pairs={{0,64},{64,0},{8,72},{72,8},{16,80},{80,16},{24,88},{88,24},{32,96... | collective-permute-start | bytes 786440 | tf_op jit(solution)/shard_map/ppermute | solution.py:21
  92.6 19.8 %collective-permute-start.11 = (bf16[2,2,256,128]{3,2,1,0:T(8,128)(2,1)S(1)}, bf16[2,2,256,128]{3,2,1,0:T(8,128)(2,1)S(1)}, u32[]{:S(2)}, u32[]{:S(2)}) collective-permute-start(bf16[2,2,256,128]{3,2,1,0:T(8,128)(2,1)S(1)} %get-tuple-element.52), channel_id=1, source_target_pairs={{0,4},{4,0},{1,5},{5,1},{2,6},{6,2},{3,7},{7,3},{8,12},{12,8},{9,1... | collective-permute-start | bytes 786440 | tf_op jit(solution)/shard_map/ppermute | solution.py:21
  98.2 15.4 %collective-permute-start.8 = (bf16[2,2,256,128]{3,2,1,0:T(8,128)(2,1)S(1)}, bf16[2,2,256,128]{3,2,1,0:T(8,128)(2,1)S(1)}, u32[]{:S(2)}, u32[]{:S(2)}) collective-permute-start(bf16[2,2,256,128]{3,2,1,0:T(8,128)(2,1)S(1)} %get-tuple-element.46), channel_id=1, source_target_pairs={{0,4},{4,0},{1,5},{5,1},{2,6},{6,2},{3,7},{7,3},{8,12},{12,8},{9,1... | collective-permute-start | bytes 786440 | tf_op jit(solution)/shard_map/ppermute | solution.py:21
  103.8 11.0 %collective-permute-start.5 = (bf16[2,2,256,128]{3,2,1,0:T(8,128)(2,1)S(1)}, bf16[2,2,256,128]{3,2,1,0:T(8,128)(2,1)S(1)}, u32[]{:S(2)}, u32[]{:S(2)}) collective-permute-start(bf16[2,2,256,128]{3,2,1,0:T(8,128)(2,1)S(1)} %get-tuple-element.40), channel_id=1, source_target_pairs={{0,4},{4,0},{1,5},{5,1},{2,6},{6,2},{3,7},{7,3},{8,12},{12,8},{9,1... | collective-permute-start | bytes 786440 | tf_op jit(solution)/shard_map/ppermute | solution.py:21
  109.5 9.4 %collective-permute-start.2 = (bf16[2,2,256,128]{3,2,1,0:T(8,128)(2,1)S(1)}, bf16[2,2,256,128]{3,2,1,0:T(8,128)(2,1)S(1)}, u32[]{:S(2)}, u32[]{:S(2)}) collective-permute-start(bf16[2,2,256,128]{3,2,1,0:T(8,128)(2,1)S(1)} %get-tuple-element.34), channel_id=1, source_target_pairs={{0,4},{4,0},{1,5},{5,1},{2,6},{6,2},{3,7},{7,3},{8,12},{12,8},{9,1... | collective-permute-start | bytes 786440 | tf_op jit(solution)/shard_map/ppermute | solution.py:21

commit v2 on v0

v2 whole, which is shorter than its diff:
```python
import functools

import jax
import jax.numpy as jnp
from jax import lax
from jax.experimental import pallas as pl
from jax.experimental.pallas import tpu as pltpu
from jax.sharding import PartitionSpec as P

HALVES = 2
PIECES = 4
FIRST_LIMIT = 62 * 1024 * 1024
SECOND_LIMIT = 54 * 1024 * 1024
LIMIT = 32 * 1024 * 1024


def partner_2(block, axis, apart):
    count = lax.axis_size(axis)
    route = []
    for low in range(count):
        high = low | 1 << apart
        if high != low and high < count:
            route += [(low, high), (high, low)]
    return lax.ppermute(block, axis, route)


def own_bit(axis, place):
    return lax.rem(lax.div(lax.axis_index(axis), 2**place), 2)


def product(blocks, vectors):
    stacked = vectors.reshape(2 * vectors.shape[1], vectors.shape[2])
    real_rows = jnp.concatenate([blocks[0], -blocks[1]], axis=1)
    imag_rows = jnp.concatenate([blocks[1], blocks[0]], axis=1)
    rows = jnp.concatenate([real_rows, imag_rows], axis=0)
    both = jnp.dot(rows, stacked, preferred_element_type=jnp.float32)
    return both.reshape(2, blocks.shape[1], vectors.shape[2])


def first_pair(target, t0, coeffs):
    own_term = product(t0[target, target], coeffs[target])
    partner = product(t0[1 - target, target], coeffs[1 - target]).astype(jnp.bfloat16)
    return (own_term + partner.astype(jnp.float32)).astype(jnp.bfloat16)


def leaf_kernel(
    start, width, place, x_hbm, l_hbm, t_hbm, a0_ref, a1_ref, p0_ref, p1_ref, x, l, t0, t1, sems
):
    other = 1 - own_bit(*place)
    columns = pl.ds(start, width)
    deep = l_hbm.shape[3] // PIECES
    nodes = l_hbm.shape[0]
    moves = []
    for b in range(nodes):
        for piece in range(PIECES):
            span = pl.ds(piece * deep, deep)
            place_at = b * PIECES + piece
            moves.append(
                (
                    pltpu.make_async_copy(
                        l_hbm.at[b, :, :, span], l.at[b, :, :, span], sems.at[2 * place_at]
                    ),
                    pltpu.make_async_copy(
                        x_hbm.at[b, :, span, columns], x.at[b, :, span], sems.at[2 * place_at + 1]
                    ),
                )
            )
    base = 2 * nodes * PIECES
    blocks_0 = pltpu.make_async_copy(t_hbm.at[0], t0, sems.at[base])
    blocks_1 = pltpu.make_async_copy(t_hbm.at[1, :, other], t1, sems.at[base + 1])
    for pair in moves:
        for move in pair:
            move.start()
    blocks_0.start()
    blocks_1.start()
    coeffs = []
    for b in range(nodes):
        total = None
        for piece in range(PIECES):
            for move in moves[b * PIECES + piece]:
                move.wait()
            span = slice(piece * deep, (piece + 1) * deep)
            term = product(l[b, :, :, span], x[b, :, span, :])
            total = term if total is None else total + term
        coeffs.append(total.astype(jnp.bfloat16))
    blocks_0.wait()
    for b, (a_ref, p_ref) in enumerate(((a0_ref, p0_ref), (a1_ref, p1_ref))):
        after = first_pair(b, t0, coeffs)
        a_ref[...] = after
        if b == 0:
            blocks_1.wait()
        p_ref[...] = product(t1[b], after).astype(jnp.bfloat16)


def middle_kernel(level, node, place, next_place, a_ref, in_ref, t_ref, a_out, p_out):
    own = own_bit(*place)
    other = 1 - own_bit(*next_place)
    own_term = product(t_ref[level, node, own], a_ref[...])
    after = (own_term + in_ref[...].astype(jnp.float32)).astype(jnp.bfloat16)
    a_out[...] = after
    p_out[...] = product(t_ref[level + 1, node, other], after).astype(jnp.bfloat16)


def last_kernel(level, node, start, width, place, a_ref, in_ref, t_ref, *refs):
    out_hbm, out, sems = refs[-3:]
    own = own_bit(*place)
    own_term = product(t_ref[level, node, own], a_ref[...])
    out[...] = (own_term + in_ref[...].astype(jnp.float32)).astype(jnp.bfloat16)
    store = pltpu.make_async_copy(out, out_hbm.at[node, :, :, pl.ds(start, width)], sems.at[0])
    store.start()
    store.wait()


def local(inputs, leaf_maps, transfer_blocks):
    nodes, _, rank, rows = leaf_maps.shape
    columns = inputs.shape[3]
    width = columns // HALVES
    src_bits = lax.axis_size("src").bit_length() - 1
    tgt_bits = lax.axis_size("tgt").bit_length() - 1
    places = [None, ("src", src_bits - 1), ("src", src_bits - 2), ("tgt", tgt_bits - 1)]

    part = jax.ShapeDtypeStruct((2, rank, width), jnp.bfloat16)
    anywhere = pl.BlockSpec(memory_space=pltpu.HBM)
    here = pl.BlockSpec(memory_space=pltpu.VMEM)

    def params(limit):
        return pltpu.CompilerParams(vmem_limit_bytes=limit)

    def cost(products):
        return pl.CostEstimate(
            flops=products, bytes_accessed=products, transcendentals=0
        )

    def leaf(half):
        return pl.pallas_call(
            functools.partial(leaf_kernel, half * width, width, places[1]),
            out_shape=(part,) * 4,
            in_specs=[anywhere] * 3,
            out_specs=(here,) * 4,
            scratch_shapes=[
                pltpu.VMEM((nodes, 2, rows, width), jnp.bfloat16),
                pltpu.VMEM((nodes, 2, rank, rows), jnp.bfloat16),
                pltpu.VMEM((nodes, 2, 2, rank, rank), jnp.bfloat16),
                pltpu.VMEM((nodes, 2, rank, rank), jnp.bfloat16),
                pltpu.SemaphoreType.DMA((2 * nodes * PIECES + 2,)),
            ],
            compiler_params=params(FIRST_LIMIT if half == 0 else SECOND_LIMIT),
            cost_estimate=cost(nodes * (rows // rank + 3)),
            name="leaf",
        )(inputs, leaf_maps, transfer_blocks)

    def middle(level, node, held, arrived):
        return pl.pallas_call(
            functools.partial(middle_kernel, level, node, places[level], places[level + 1]),
            out_shape=(part, part),
            in_specs=[here] * 3,
            out_specs=(here, here),
            compiler_params=params(LIMIT),
            cost_estimate=cost(2),
            name="middle",
        )(held, arrived, transfer_blocks)

    def last(level, node, half, held, arrived, result):
        operands = (held, arrived, transfer_blocks)
        aliases = {}
        if result is not None:
            operands += (result,)
            aliases = {3: 0}
        return pl.pallas_call(
            functools.partial(last_kernel, level, node, half * width, width, places[level]),
            out_shape=jax.ShapeDtypeStruct((nodes, 2, rank, columns), jnp.bfloat16),
            in_specs=[here] * 3 + [anywhere] * len(aliases),
            out_specs=anywhere,
            scratch_shapes=[
                pltpu.VMEM((2, rank, width), jnp.bfloat16),
                pltpu.SemaphoreType.DMA((1,)),
            ],
            input_output_aliases=aliases,
            compiler_params=params(LIMIT),
            cost_estimate=cost(1),
            name="last",
        )(*operands)

    chunks = [(half, node) for half in range(HALVES) for node in range(nodes)]
    held, flying = {}, {}

    for half in range(HALVES):
        results = leaf(half)
        for node in range(nodes):
            held[half, node] = results[node]
            flying[half, node] = partner_2(results[nodes + node], *places[1])
    for level in (1, 2):
        for half, node in chunks:
            held[half, node], sent = middle(level, node, held[half, node], flying[half, node])
            flying[half, node] = partner_2(sent, *places[level + 1])
    result = None
    for half, node in chunks:
        result = last(3, node, half, held[half, node], flying[half, node], result)
    return result


def solution(mesh):
    placed = (
        P(("src", "tgt"), None, None, None),
        P(("src", "tgt"), None, None, None),
        P(None, ("src", "tgt"), None, None, None, None),
    )
    return jax.shard_map(
        local,
        mesh=mesh,
        in_specs=placed,
        out_specs=P(("src", "tgt"), None, None, None),
        check_vma=False,
    )
```

time: 157 us -> 117 us (0.75); the launches traced: 155 us -> 117 us
  waiting for transfers between devices: 89.7 us -> 34.6 us
  starting transfers between devices: 29.4 us -> 60 us
  matrix products: 24.4 us -> 0 us
  Pallas kernels: 0 us -> 22.2 us
  local copies, waits for them, and re-layouts: 7.3 us -> 0.02 us
  other arithmetic: 4 us -> 0 us
    ppermute x3 -> x12, waiting for transfers between devices: 89.7 us -> 34.6 us  [partner_2(): return lax.ppermute(block, axis, route)]
    ppermute x3 -> x12, starting transfers between devices: 29.4 us -> 60 us  [partner_2(): return lax.ppermute(block, axis, route)]
    dot_general x44 -> x0, matrix products: 24.4 us -> none  [batched(): jnp.einsum('nij,njr->nir', left_side, right_side, preferred_element_type=...]
    pallas_call x0 -> x14, Pallas kernels: none -> 22.2 us  [the longest x2 12.3 us: leaf(): pl.pallas_call(functools.partial(leaf_kernel, half * width, width, places...]
    unnamed x38 -> x10, local copies, waits for them, and re-layouts: 3.59 us -> 0.02 us
    convert_element_type x3 -> x0, other arithmetic: 2.31 us -> none  [butterfly_level(): (local_term + remote_term(coeffs, other_blocks, axis_src, bit_place)).ast...]
    another operation x4 -> x0, other arithmetic: 1.6 us -> none  [the longest x3 1.3 us: complex_product(): return jnp.stack([real_part, imag_part], axis=1)]
  transfers between devices with their start and end apart: 3 -> 12, of which waited for: 3 -> 5; matrix products, arithmetic and copies ran while one was open for 3% -> 0% of each run, Pallas kernels for 0% -> 13%
where the time goes in v2:
time: 117 us
  starting transfers between devices  60 us (51%)
  waiting for transfers between devices  34.6 us (30%)
  Pallas kernels  22.2 us (19%)
    ppermute x12, starting transfers between devices, partner_2(): return lax.ppermute(block, axis, route)  60 us
    ppermute x12, waiting for transfers between devices, partner_2(): return lax.ppermute(block, axis, route)  34.6 us
    pallas_call x2, Pallas kernels, leaf(): pl.pallas_call(functools.partial(leaf_kernel, half * width, width, places...  12.3 us
    pallas_call x8, Pallas kernels, middle(): pl.pallas_call(functools.partial(middle_kernel, level, node, places[level...  5.89 us
    pallas_call x4, Pallas kernels, last(): pl.pallas_call(functools.partial(last_kernel, level, node, half * width,...  4.04 us
  transfers between devices with their start and end apart: 12, of which 5 were waited for; matrix products, arithmetic and copies ran while one was open for 0% of the time, Pallas kernels for 13%

profile of v2, /device:TPU:1, one launch (start us, length us, event | category | flops | bytes accessed | tf_op | source)
XLA Modules:
  0.0 117.1 jit_solution(2870483794781666807)
XLA Ops:
  0.0 6.1 %leaf.3 = (bf16[2,256,256]{2,1,0:T(8,128)(2,1)}, bf16[2,256,256]{2,1,0:T(8,128)(2,1)}, bf16[2,256,256]{2,1,0:T(8,128)(2,1)}, bf16[2,256,256]{2,1,0:T(8,128)(2,1)}) custom-call(bf16[2,2,1024,512]{3,2,1,0:T(8,128)(2,1)} %x_hbm.3, bf16[2,2,256,1024]{3,2,1,0:T(8,128)(2,1)} %l_hbm.3, bf16[4,2,2,2,256,256]{5,4,3,2,1,0:T(8,128)(2,1)} %t_ref.23), custom_call_target="tpu_custom_call" | custom-call | flops 14 | bytes 14 | tf_op jit(solution)/shard_map/leaf/pallas_call | solution.py:135
  6.1 7.8 %collective-permute-start.6 = (bf16[2,256,256]{2,1,0:T(8,128)(2,1)}, bf16[2,256,256]{2,1,0:T(8,128)(2,1)S(1)}, u32[]{:S(2)}, u32[]{:S(2)}) collective-permute-start(bf16[2,256,256]{2,1,0:T(8,128)(2,1)} %get-tuple-element.42), channel_id=1, source_target_pairs={{0,128},{128,0},{8,136},{136,8},{16,144},{144,16},{24,152},{152,24... | collective-permute-start | bytes 786440 | tf_op jit(solution)/shard_map/ppermute | solution.py:24
  13.9 0.0 copy-start
  13.9 0.0 copy-start.4
  13.9 0.1 collective-permute-start.9
  14.0 6.2 %leaf.2 = (bf16[2,256,256]{2,1,0:T(8,128)(2,1)}, bf16[2,256,256]{2,1,0:T(8,128)(2,1)}, bf16[2,256,256]{2,1,0:T(8,128)(2,1)}, bf16[2,256,256]{2,1,0:T(8,128)(2,1)}) custom-call(bf16[2,2,1024,512]{3,2,1,0:T(8,128)(2,1)} %x_hbm.3, bf16[2,2,256,1024]{3,2,1,0:T(8,128)(2,1)} %l_hbm.3, bf16[4,2,2,2,256,256]{5,4,3,2,1,0:T(8,128)(2,1)} %t_ref.23), custom_call_target="tpu_custom_call" | custom-call | flops 14 | bytes 14 | tf_op jit(solution)/shard_map/leaf/pallas_call | solution.py:135
  20.2 0.0 copy-start.3
  20.2 5.2 %collective-permute-start.3 = (bf16[2,256,256]{2,1,0:T(8,128)(2,1)}, bf16[2,256,256]{2,1,0:T(8,128)(2,1)S(1)}, u32[]{:S(2)}, u32[]{:S(2)}) collective-permute-start(bf16[2,256,256]{2,1,0:T(8,128)(2,1)} %get-tuple-element.36), channel_id=1, source_target_pairs={{0,128},{128,0},{8,136},{136,8},{16,144},{144,16},{24,152},{152,24... | collective-permute-start | bytes 786440 | tf_op jit(solution)/shard_map/ppermute | solution.py:24
  25.4 0.3 collective-permute-start
  25.7 0.0 collective-permute-done.6.in_ref
  25.7 0.0 copy-done
  25.7 0.0 copy-done.4
  25.7 0.0 copy-start.2
  25.7 0.7 middle.12
  26.5 12.8 %collective-permute-start.7 = (bf16[2,256,256]{2,1,0:T(8,128)(2,1)S(1)}, bf16[2,256,256]{2,1,0:T(8,128)(2,1)S(1)}, u32[]{:S(2)}, u32[]{:S(2)}) collective-permute-start(bf16[2,256,256]{2,1,0:T(8,128)(2,1)S(1)} %get-tuple-element.44), channel_id=1, source_target_pairs={{0,64},{64,0},{8,72},{72,8},{16,80},{80,16},{24,88},{88,24},{32,96... | collective-permute-start | bytes 786440 | tf_op jit(solution)/shard_map/ppermute | solution.py:24
  39.2 0.0 collective-permute-done.9.in_ref
  39.2 0.0 copy-done.3
  39.2 0.0 copy-start.1
  39.2 0.7 middle.14
  40.0 11.9 %collective-permute-start.10 = (bf16[2,256,256]{2,1,0:T(8,128)(2,1)S(1)}, bf16[2,256,256]{2,1,0:T(8,128)(2,1)S(1)}, u32[]{:S(2)}, u32[]{:S(2)}) collective-permute-start(bf16[2,256,256]{2,1,0:T(8,128)(2,1)S(1)} %get-tuple-element.50), channel_id=1, source_target_pairs={{0,64},{64,0},{8,72},{72,8},{16,80},{80,16},{24,88},{88,24},{32,96... | collective-permute-start | bytes 786440 | tf_op jit(solution)/shard_map/ppermute | solution.py:24
  51.9 0.0 collective-permute-done.3.in_ref
  51.9 0.0 copy-done.2
  51.9 0.7 middle.10
  52.6 4.9 %collective-permute-start.4 = (bf16[2,256,256]{2,1,0:T(8,128)(2,1)S(1)}, bf16[2,256,256]{2,1,0:T(8,128)(2,1)S(1)}, u32[]{:S(2)}, u32[]{:S(2)}) collective-permute-start(bf16[2,256,256]{2,1,0:T(8,128)(2,1)S(1)} %get-tuple-element.38), channel_id=1, source_target_pairs={{0,64},{64,0},{8,72},{72,8},{16,80},{80,16},{24,88},{88,24},{32,96... | collective-permute-start | bytes 786440 | tf_op jit(solution)/shard_map/ppermute | solution.py:24
  57.5 0.0 collective-permute-done.in_ref
  57.5 0.0 copy-done.1
  57.5 0.7 middle.8
  58.2 4.9 %collective-permute-start.1 = (bf16[2,256,256]{2,1,0:T(8,128)(2,1)S(1)}, bf16[2,256,256]{2,1,0:T(8,128)(2,1)S(1)}, u32[]{:S(2)}, u32[]{:S(2)}) collective-permute-start(bf16[2,256,256]{2,1,0:T(8,128)(2,1)S(1)} %get-tuple-element.32), channel_id=1, source_target_pairs={{0,64},{64,0},{8,72},{72,8},{16,80},{80,16},{24,88},{88,24},{32,96... | collective-permute-start | bytes 786440 | tf_op jit(solution)/shard_map/ppermute | solution.py:24
  63.1 25.9 %collective-permute-done.7.in_ref = bf16[2,256,256]{2,1,0:T(8,128)(2,1)S(1)} collective-permute-done((bf16[2,256,256]{2,1,0:T(8,128)(2,1)S(1)}, bf16[2,256,256]{2,1,0:T(8,128)(2,1)S(1)}, u32[]{:S(2)}, u32[]{:S(2)}) %collective-permute-start.7) | collective-permute-done | bytes 262176 | tf_op jit(solution)/shard_map/ppermute | solution.py:24
  89.0 0.7 middle.13
  89.7 3.2 %collective-permute-start.8 = (bf16[2,256,256]{2,1,0:T(8,128)(2,1)S(1)}, bf16[2,256,256]{2,1,0:T(8,128)(2,1)S(1)}, u32[]{:S(2)}, u32[]{:S(2)}) collective-permute-start(bf16[2,256,256]{2,1,0:T(8,128)(2,1)S(1)} %get-tuple-element.46), channel_id=1, source_target_pairs={{0,4},{4,0},{1,5},{5,1},{2,6},{6,2},{3,7},{7,3},{8,12},{12,8},{9,1... | collective-permute-start | bytes 786440 | tf_op jit(solution)/shard_map/ppermute | solution.py:24
  92.9 1.7 %collective-permute-done.10.in_ref = bf16[2,256,256]{2,1,0:T(8,128)(2,1)S(1)} collective-permute-done((bf16[2,256,256]{2,1,0:T(8,128)(2,1)S(1)}, bf16[2,256,256]{2,1,0:T(8,128)(2,1)S(1)}, u32[]{:S(2)}, u32[]{:S(2)}) %collective-permute-start.10) | collective-permute-done | bytes 262176 | tf_op jit(solution)/shard_map/ppermute | solution.py:24
  94.6 0.7 middle.15
  95.3 3.0 %collective-permute-start.11 = (bf16[2,256,256]{2,1,0:T(8,128)(2,1)S(1)}, bf16[2,256,256]{2,1,0:T(8,128)(2,1)S(1)}, u32[]{:S(2)}, u32[]{:S(2)}) collective-permute-start(bf16[2,256,256]{2,1,0:T(8,128)(2,1)S(1)} %get-tuple-element.52), channel_id=1, source_target_pairs={{0,4},{4,0},{1,5},{5,1},{2,6},{6,2},{3,7},{7,3},{8,12},{12,8},{9,1... | collective-permute-start | bytes 786440 | tf_op jit(solution)/shard_map/ppermute | solution.py:24
  98.3 1.9 %collective-permute-done.4.in_ref = bf16[2,256,256]{2,1,0:T(8,128)(2,1)S(1)} collective-permute-done((bf16[2,256,256]{2,1,0:T(8,128)(2,1)S(1)}, bf16[2,256,256]{2,1,0:T(8,128)(2,1)S(1)}, u32[]{:S(2)}, u32[]{:S(2)}) %collective-permute-start.4) | collective-permute-done | bytes 262176 | tf_op jit(solution)/shard_map/ppermute | solution.py:24
  100.2 0.7 middle.11
  100.9 3.0 %collective-permute-start.5 = (bf16[2,256,256]{2,1,0:T(8,128)(2,1)S(1)}, bf16[2,256,256]{2,1,0:T(8,128)(2,1)S(1)}, u32[]{:S(2)}, u32[]{:S(2)}) collective-permute-start(bf16[2,256,256]{2,1,0:T(8,128)(2,1)S(1)} %get-tuple-element.40), channel_id=1, source_target_pairs={{0,4},{4,0},{1,5},{5,1},{2,6},{6,2},{3,7},{7,3},{8,12},{12,8},{9,1... | collective-permute-start | bytes 786440 | tf_op jit(solution)/shard_map/ppermute | solution.py:24
  103.9 1.9 %collective-permute-done.1.in_ref = bf16[2,256,256]{2,1,0:T(8,128)(2,1)S(1)} collective-permute-done((bf16[2,256,256]{2,1,0:T(8,128)(2,1)S(1)}, bf16[2,256,256]{2,1,0:T(8,128)(2,1)S(1)}, u32[]{:S(2)}, u32[]{:S(2)}) %collective-permute-start.1) | collective-permute-done | bytes 262176 | tf_op jit(solution)/shard_map/ppermute | solution.py:24
  105.8 0.7 middle.9
  106.6 3.0 %collective-permute-start.2 = (bf16[2,256,256]{2,1,0:T(8,128)(2,1)S(1)}, bf16[2,256,256]{2,1,0:T(8,128)(2,1)S(1)}, u32[]{:S(2)}, u32[]{:S(2)}) collective-permute-start(bf16[2,256,256]{2,1,0:T(8,128)(2,1)S(1)} %get-tuple-element.34), channel_id=1, source_target_pairs={{0,4},{4,0},{1,5},{5,1},{2,6},{6,2},{3,7},{7,3},{8,12},{12,8},{9,1... | collective-permute-start | bytes 786440 | tf_op jit(solution)/shard_map/ppermute | solution.py:24
  109.6 0.0 collective-permute-done.11.in_ref
  109.6 1.0 last.4.refs_0_
  110.6 0.0 collective-permute-done.8.in_ref
  110.6 1.0 last.5.refs_0_
  111.6 0.0 collective-permute-done.5.in_ref
  111.6 1.0 last.6.refs_0_
  112.6 3.2 %collective-permute-done.2.in_ref = bf16[2,256,256]{2,1,0:T(8,128)(2,1)S(1)} collective-permute-done((bf16[2,256,256]{2,1,0:T(8,128)(2,1)S(1)}, bf16[2,256,256]{2,1,0:T(8,128)(2,1)S(1)}, u32[]{:S(2)}, u32[]{:S(2)}) %collective-permute-start.2) | collective-permute-done | bytes 262176 | tf_op jit(solution)/shard_map/ppermute | solution.py:24
  115.9 1.0 last.7
Async XLA Ops:
  6.1 19.6 %collective-permute-start.6 = (bf16[2,256,256]{2,1,0:T(8,128)(2,1)}, bf16[2,256,256]{2,1,0:T(8,128)(2,1)S(1)}, u32[]{:S(2)}, u32[]{:S(2)}) collective-permute-start(bf16[2,256,256]{2,1,0:T(8,128)(2,1)} %get-tuple-element.42), channel_id=1, source_target_pairs={{0,128},{128,0},{8,136},{136,8},{16,144},{144,16},{24,152},{152,24... | collective-permute-start | bytes 786440 | tf_op jit(solution)/shard_map/ppermute | solution.py:24
  13.9 11.8 %copy-start = (bf16[4,2,2,2,256,256]{5,4,3,2,1,0:T(8,128)(2,1)S(1)}, bf16[4,2,2,2,256,256]{5,4,3,2,1,0:T(8,128)(2,1)}, u32[]{:S(2)}) copy-start(bf16[4,2,2,2,256,256]{5,4,3,2,1,0:T(8,128)(2,1)} %t_ref.23) | copy-start | bytes 12582916
  13.9 11.8 %copy-start.4 = (bf16[2,256,256]{2,1,0:T(8,128)(2,1)S(1)}, bf16[2,256,256]{2,1,0:T(8,128)(2,1)}, u32[]{:S(2)}) copy-start(bf16[2,256,256]{2,1,0:T(8,128)(2,1)} %get-tuple-element.41.a_ref) | copy-start | bytes 786436
  13.9 25.3 %collective-permute-start.9 = (bf16[2,256,256]{2,1,0:T(8,128)(2,1)}, bf16[2,256,256]{2,1,0:T(8,128)(2,1)S(1)}, u32[]{:S(2)}, u32[]{:S(2)}) collective-permute-start(bf16[2,256,256]{2,1,0:T(8,128)(2,1)} %get-tuple-element.48), channel_id=1, source_target_pairs={{0,128},{128,0},{8,136},{136,8},{16,144},{144,16},{24,152},{152,24... | collective-permute-start | bytes 786440 | tf_op jit(solution)/shard_map/ppermute | solution.py:24
  20.2 19.0 %copy-start.3 = (bf16[2,256,256]{2,1,0:T(8,128)(2,1)S(1)}, bf16[2,256,256]{2,1,0:T(8,128)(2,1)}, u32[]{:S(2)}) copy-start(bf16[2,256,256]{2,1,0:T(8,128)(2,1)} %get-tuple-element.47.a_ref) | copy-start | bytes 786436
  20.2 31.7 %collective-permute-start.3 = (bf16[2,256,256]{2,1,0:T(8,128)(2,1)}, bf16[2,256,256]{2,1,0:T(8,128)(2,1)S(1)}, u32[]{:S(2)}, u32[]{:S(2)}) collective-permute-start(bf16[2,256,256]{2,1,0:T(8,128)(2,1)} %get-tuple-element.36), channel_id=1, source_target_pairs={{0,128},{128,0},{8,136},{136,8},{16,144},{144,16},{24,152},{152,24... | collective-permute-start | bytes 786440 | tf_op jit(solution)/shard_map/ppermute | solution.py:24
  25.4 32.1 %collective-permute-start = (bf16[2,256,256]{2,1,0:T(8,128)(2,1)}, bf16[2,256,256]{2,1,0:T(8,128)(2,1)S(1)}, u32[]{:S(2)}, u32[]{:S(2)}) collective-permute-start(bf16[2,256,256]{2,1,0:T(8,128)(2,1)} %get-tuple-element.30), channel_id=1, source_target_pairs={{0,128},{128,0},{8,136},{136,8},{16,144},{144,16},{24,152},{152,24... | collective-permute-start | bytes 786440 | tf_op jit(solution)/shard_map/ppermute | solution.py:24
  25.7 26.2 %copy-start.2 = (bf16[2,256,256]{2,1,0:T(8,128)(2,1)S(1)}, bf16[2,256,256]{2,1,0:T(8,128)(2,1)}, u32[]{:S(2)}) copy-start(bf16[2,256,256]{2,1,0:T(8,128)(2,1)} %get-tuple-element.35.a_ref) | copy-start | bytes 786436
  26.5 62.5 %collective-permute-start.7 = (bf16[2,256,256]{2,1,0:T(8,128)(2,1)S(1)}, bf16[2,256,256]{2,1,0:T(8,128)(2,1)S(1)}, u32[]{:S(2)}, u32[]{:S(2)}) collective-permute-start(bf16[2,256,256]{2,1,0:T(8,128)(2,1)S(1)} %get-tuple-element.44), channel_id=1, source_target_pairs={{0,64},{64,0},{8,72},{72,8},{16,80},{80,16},{24,88},{88,24},{32,96... | collective-permute-start | bytes 786440 | tf_op jit(solution)/shard_map/ppermute | solution.py:24
  39.2 18.3 %copy-start.1 = (bf16[2,256,256]{2,1,0:T(8,128)(2,1)S(1)}, bf16[2,256,256]{2,1,0:T(8,128)(2,1)}, u32[]{:S(2)}) copy-start(bf16[2,256,256]{2,1,0:T(8,128)(2,1)} %get-tuple-element.29.a_ref) | copy-start | bytes 786436
  40.0 54.6 %collective-permute-start.10 = (bf16[2,256,256]{2,1,0:T(8,128)(2,1)S(1)}, bf16[2,256,256]{2,1,0:T(8,128)(2,1)S(1)}, u32[]{:S(2)}, u32[]{:S(2)}) collective-permute-start(bf16[2,256,256]{2,1,0:T(8,128)(2,1)S(1)} %get-tuple-element.50), channel_id=1, source_target_pairs={{0,64},{64,0},{8,72},{72,8},{16,80},{80,16},{24,88},{88,24},{32,96... | collective-permute-start | bytes 786440 | tf_op jit(solution)/shard_map/ppermute | solution.py:24
  52.6 47.6 %collective-permute-start.4 = (bf16[2,256,256]{2,1,0:T(8,128)(2,1)S(1)}, bf16[2,256,256]{2,1,0:T(8,128)(2,1)S(1)}, u32[]{:S(2)}, u32[]{:S(2)}) collective-permute-start(bf16[2,256,256]{2,1,0:T(8,128)(2,1)S(1)} %get-tuple-element.38), channel_id=1, source_target_pairs={{0,64},{64,0},{8,72},{72,8},{16,80},{80,16},{24,88},{88,24},{32,96... | collective-permute-start | bytes 786440 | tf_op jit(solution)/shard_map/ppermute | solution.py:24
  58.2 47.6 %collective-permute-start.1 = (bf16[2,256,256]{2,1,0:T(8,128)(2,1)S(1)}, bf16[2,256,256]{2,1,0:T(8,128)(2,1)S(1)}, u32[]{:S(2)}, u32[]{:S(2)}) collective-permute-start(bf16[2,256,256]{2,1,0:T(8,128)(2,1)S(1)} %get-tuple-element.32), channel_id=1, source_target_pairs={{0,64},{64,0},{8,72},{72,8},{16,80},{80,16},{24,88},{88,24},{32,96... | collective-permute-start | bytes 786440 | tf_op jit(solution)/shard_map/ppermute | solution.py:24
  89.7 20.9 %collective-permute-start.8 = (bf16[2,256,256]{2,1,0:T(8,128)(2,1)S(1)}, bf16[2,256,256]{2,1,0:T(8,128)(2,1)S(1)}, u32[]{:S(2)}, u32[]{:S(2)}) collective-permute-start(bf16[2,256,256]{2,1,0:T(8,128)(2,1)S(1)} %get-tuple-element.46), channel_id=1, source_target_pairs={{0,4},{4,0},{1,5},{5,1},{2,6},{6,2},{3,7},{7,3},{8,12},{12,8},{9,1... | collective-permute-start | bytes 786440 | tf_op jit(solution)/shard_map/ppermute | solution.py:24
  95.3 14.2 %collective-permute-start.11 = (bf16[2,256,256]{2,1,0:T(8,128)(2,1)S(1)}, bf16[2,256,256]{2,1,0:T(8,128)(2,1)S(1)}, u32[]{:S(2)}, u32[]{:S(2)}) collective-permute-start(bf16[2,256,256]{2,1,0:T(8,128)(2,1)S(1)} %get-tuple-element.52), channel_id=1, source_target_pairs={{0,4},{4,0},{1,5},{5,1},{2,6},{6,2},{3,7},{7,3},{8,12},{12,8},{9,1... | collective-permute-start | bytes 786440 | tf_op jit(solution)/shard_map/ppermute | solution.py:24
  100.9 10.7 %collective-permute-start.5 = (bf16[2,256,256]{2,1,0:T(8,128)(2,1)S(1)}, bf16[2,256,256]{2,1,0:T(8,128)(2,1)S(1)}, u32[]{:S(2)}, u32[]{:S(2)}) collective-permute-start(bf16[2,256,256]{2,1,0:T(8,128)(2,1)S(1)} %get-tuple-element.40), channel_id=1, source_target_pairs={{0,4},{4,0},{1,5},{5,1},{2,6},{6,2},{3,7},{7,3},{8,12},{12,8},{9,1... | collective-permute-start | bytes 786440 | tf_op jit(solution)/shard_map/ppermute | solution.py:24
  106.6 9.3 %collective-permute-start.2 = (bf16[2,256,256]{2,1,0:T(8,128)(2,1)S(1)}, bf16[2,256,256]{2,1,0:T(8,128)(2,1)S(1)}, u32[]{:S(2)}, u32[]{:S(2)}) collective-permute-start(bf16[2,256,256]{2,1,0:T(8,128)(2,1)S(1)} %get-tuple-element.34), channel_id=1, source_target_pairs={{0,4},{4,0},{1,5},{5,1},{2,6},{6,2},{3,7},{7,3},{8,12},{12,8},{9,1... | collective-permute-start | bytes 786440 | tf_op jit(solution)/shard_map/ppermute | solution.py:24

commit v3 on v2

v3 whole, which is shorter than its diff:
```python
import functools

import jax
import jax.numpy as jnp
from jax import lax
from jax.experimental import pallas as pl
from jax.experimental.pallas import tpu as pltpu
from jax.sharding import PartitionSpec as P

GROUPS = ((128, False), (128, False), (128, False), (128, False))
LEAF_LIMIT = 24 * 1024 * 1024
LIMIT = 16 * 1024 * 1024


def partner_2(block, axis, apart):
    count = lax.axis_size(axis)
    route = []
    for low in range(count):
        high = low | 1 << apart
        if high != low and high < count:
            route += [(low, high), (high, low)]
    return lax.ppermute(block, axis, route)


def own_bit(axis, place):
    return lax.rem(lax.div(lax.axis_index(axis), 2**place), 2)


def product(blocks, vectors):
    rank, width = blocks.shape[1], vectors.shape[2]
    if width >= 256:
        stacked = vectors.reshape(2 * vectors.shape[1], width)
        real_rows = jnp.concatenate([blocks[0], -blocks[1]], axis=1)
        imag_rows = jnp.concatenate([blocks[1], blocks[0]], axis=1)
        rows = jnp.concatenate([real_rows, imag_rows], axis=0)
        both = jnp.dot(rows, stacked, preferred_element_type=jnp.float32)
        return both.reshape(2, rank, width)
    rows = blocks.reshape(2 * rank, blocks.shape[2])
    beside = jnp.concatenate([vectors[0], vectors[1]], axis=1)
    all_four = jnp.dot(rows, beside, preferred_element_type=jnp.float32)
    real_part = all_four[:rank, :width] - all_four[rank:, width:]
    imag_part = all_four[:rank, width:] + all_four[rank:, :width]
    return jnp.stack([real_part, imag_part])


def leaf_kernel(start, width, apart, place, x_hbm, l_hbm, t_hbm, *refs):
    nodes = l_hbm.shape[0]
    outs, (x, l, t0, t1, sems) = refs[:-5], refs[-5:]
    if apart:
        a_refs, p_refs = [ref.at[0] for ref in outs[:nodes]], [ref.at[0] for ref in outs[nodes:]]
    else:
        a_refs, p_refs = [[ref.at[b] for b in range(nodes)] for ref in outs]
    other = 1 - own_bit(*place)
    columns = pl.ds(start, width)
    moves = []
    for b in range(nodes):
        moves.append(
            (
                pltpu.make_async_copy(x_hbm.at[b, :, :, columns], x.at[b], sems.at[2 * b]),
                pltpu.make_async_copy(l_hbm.at[b], l.at[b], sems.at[2 * b + 1]),
            )
        )
    blocks_0 = pltpu.make_async_copy(t_hbm.at[0], t0, sems.at[2 * nodes])
    blocks_1 = pltpu.make_async_copy(t_hbm.at[1, :, other], t1, sems.at[2 * nodes + 1])
    for pair in moves:
        for move in pair:
            move.start()
    blocks_0.start()
    blocks_1.start()
    coeffs = []
    for b in range(nodes):
        for move in moves[b]:
            move.wait()
        coeffs.append(product(l[b], x[b]).astype(jnp.bfloat16))
    blocks_0.wait()
    for b in range(nodes):
        own_term = product(t0[b, b], coeffs[b])
        partner = product(t0[1 - b, b], coeffs[1 - b]).astype(jnp.bfloat16)
        after = (own_term + partner.astype(jnp.float32)).astype(jnp.bfloat16)
        a_refs[b][...] = after
        if b == 0:
            blocks_1.wait()
        p_refs[b][...] = product(t1[b], after).astype(jnp.bfloat16)


def middle_kernel(level, nodes, place, next_place, a_ref, in_ref, t_ref, a_out, p_out):
    own = own_bit(*place)
    other = 1 - own_bit(*next_place)
    for at, node in enumerate(nodes):
        own_term = product(t_ref[level, node, own], a_ref[at])
        after = (own_term + in_ref[at].astype(jnp.float32)).astype(jnp.bfloat16)
        a_out[at] = after
        p_out[at] = product(t_ref[level + 1, node, other], after).astype(jnp.bfloat16)


def last_kernel(level, nodes, start, width, place, a_ref, in_ref, t_ref, *refs):
    out_hbm, out, sems = refs[-3:]
    own = own_bit(*place)
    stores = []
    for at, node in enumerate(nodes):
        own_term = product(t_ref[level, node, own], a_ref[at])
        out[at] = (own_term + in_ref[at].astype(jnp.float32)).astype(jnp.bfloat16)
        stores.append(
            pltpu.make_async_copy(
                out.at[at], out_hbm.at[node, :, :, pl.ds(start, width)], sems.at[at]
            )
        )
        stores[at].start()
    for store in stores:
        store.wait()


def local(inputs, leaf_maps, transfer_blocks):
    nodes, _, rank, rows = leaf_maps.shape
    columns = inputs.shape[3]
    src_bits = lax.axis_size("src").bit_length() - 1
    tgt_bits = lax.axis_size("tgt").bit_length() - 1
    places = [None, ("src", src_bits - 1), ("src", src_bits - 2), ("tgt", tgt_bits - 1)]
    everyone = tuple(range(nodes))
    widths = [width for width, _ in GROUPS]
    starts = [sum(widths[:group]) for group in range(len(GROUPS))]
    chunks = []
    for group, (_, apart) in enumerate(GROUPS):
        chunks += [(group, (node,)) for node in everyone] if apart else [(group, everyone)]

    anywhere = pl.BlockSpec(memory_space=pltpu.HBM)
    here = pl.BlockSpec(memory_space=pltpu.VMEM)
    in_hbm = [
        pltpu.with_memory_space_constraint(array, pltpu.HBM)
        for array in (inputs, leaf_maps, transfer_blocks)
    ]
    cost = pl.CostEstimate(flops=2, bytes_accessed=2, transcendentals=0)

    def params(limit):
        return pltpu.CompilerParams(vmem_limit_bytes=limit)

    def part(group, some):
        return jax.ShapeDtypeStruct((len(some), 2, rank, widths[group]), jnp.bfloat16)

    def leaf(group):
        width, apart = GROUPS[group]
        mine = [some for at, some in chunks if at == group]
        return pl.pallas_call(
            functools.partial(leaf_kernel, starts[group], width, apart, places[1]),
            out_shape=tuple(part(group, some) for some in mine) * 2,
            in_specs=[anywhere] * 3,
            out_specs=(here,) * (2 * len(mine)),
            scratch_shapes=[
                pltpu.VMEM((nodes, 2, rows, width), jnp.bfloat16),
                pltpu.VMEM((nodes, 2, rank, rows), jnp.bfloat16),
                pltpu.VMEM((nodes, 2, 2, rank, rank), jnp.bfloat16),
                pltpu.VMEM((nodes, 2, rank, rank), jnp.bfloat16),
                pltpu.SemaphoreType.DMA((2 * nodes + 2,)),
            ],
            compiler_params=params(LEAF_LIMIT),
            cost_estimate=cost,
            name="leaf",
        )(*in_hbm)

    def middle(level, chunk, held, arrived):
        group, some = chunk
        return pl.pallas_call(
            functools.partial(middle_kernel, level, some, places[level], places[level + 1]),
            out_shape=(part(group, some),) * 2,
            in_specs=[here] * 3,
            out_specs=(here, here),
            compiler_params=params(LIMIT),
            cost_estimate=cost,
            name="middle",
        )(held, arrived, transfer_blocks)

    def last(level, chunk, held, arrived, result):
        group, some = chunk
        operands = (held, arrived, transfer_blocks)
        aliases = {}
        if result is not None:
            operands += (result,)
            aliases = {3: 0}
        return pl.pallas_call(
            functools.partial(
                last_kernel, level, some, starts[group], widths[group], places[level]
            ),
            out_shape=jax.ShapeDtypeStruct((nodes, 2, rank, columns), jnp.bfloat16),
            in_specs=[here] * 3 + [anywhere] * len(aliases),
            out_specs=anywhere,
            scratch_shapes=[
                pltpu.VMEM((len(some), 2, rank, widths[group]), jnp.bfloat16),
                pltpu.SemaphoreType.DMA((len(some),)),
            ],
            input_output_aliases=aliases,
            compiler_params=params(LIMIT),
            cost_estimate=cost,
            name="last",
        )(*operands)

    held, flying = {}, {}
    for group in range(len(GROUPS)):
        mine = [chunk for chunk in chunks if chunk[0] == group]
        results = leaf(group)
        for at, chunk in enumerate(mine):
            held[chunk] = results[at]
            flying[chunk] = partner_2(results[len(mine) + at], *places[1])
    for level in (1, 2):
        for chunk in chunks:
            held[chunk], term = middle(level, chunk, held[chunk], flying[chunk])
            flying[chunk] = partner_2(term, *places[level + 1])
    result = None
    for chunk in chunks:
        result = last(3, chunk, held[chunk], flying[chunk], result)
    return result


def solution(mesh):
    placed = (
        P(("src", "tgt"), None, None, None),
        P(("src", "tgt"), None, None, None),
        P(None, ("src", "tgt"), None, None, None, None),
    )
    return jax.shard_map(
        local,
        mesh=mesh,
        in_specs=placed,
        out_specs=P(("src", "tgt"), None, None, None),
        check_vma=False,
    )
```

time: 117 us -> 114 us (0.974)
  starting transfers between devices: 60 us -> 27.9 us
  waiting for transfers between devices: 34.6 us -> 61.2 us
  Pallas kernels: 22.2 us -> 24.8 us
    ppermute x12, starting transfers between devices: 60 us -> 27.9 us  [partner_2(): return lax.ppermute(block, axis, route)]
    ppermute x12, waiting for transfers between devices: 34.6 us -> 61.2 us  [partner_2(): return lax.ppermute(block, axis, route)]
    pallas_call x14 -> x16, Pallas kernels: 22.2 us -> 24.8 us  [the longest x4 15.3 us: leaf(): pl.pallas_call(functools.partial(leaf_kernel, starts[group], width, apart...]
  transfers between devices with their start and end apart: 12 -> 12, of which waited for: 5 -> 8; matrix products, arithmetic and copies ran while one was open for 0% -> 0% of each run, Pallas kernels for 13% -> 17%
where the time goes in v3:
time: 114 us
  waiting for transfers between devices  61.2 us (54%)
  starting transfers between devices  27.9 us (24%)
  Pallas kernels  24.8 us (22%)
    ppermute x12, waiting for transfers between devices, partner_2(): return lax.ppermute(block, axis, route)  61.2 us
    ppermute x12, starting transfers between devices, partner_2(): return lax.ppermute(block, axis, route)  27.9 us
    pallas_call x4, Pallas kernels, leaf(): pl.pallas_call(functools.partial(leaf_kernel, starts[group], width, apart...  15.3 us
    pallas_call x8, Pallas kernels, middle(): pl.pallas_call(functools.partial(middle_kernel, level, some, places[level...  5.38 us
    pallas_call x4, Pallas kernels, last(): pl.pallas_call(functools.partial(last_kernel, level, some, starts[group],...  4.07 us
  transfers between devices with their start and end apart: 12, of which 8 were waited for; matrix products, arithmetic and copies ran while one was open for 0% of the time, Pallas kernels for 17%

profile of v3, /device:TPU:1, one launch (start us, length us, event | category | flops | bytes accessed | tf_op | source)
XLA Modules:
  0.0 114.2 jit_solution(6795952062992505138)
XLA Ops:
  0.0 3.8 %leaf.7 = (bf16[2,2,256,128]{3,2,1,0:T(8,128)(2,1)S(1)}, bf16[2,2,256,128]{3,2,1,0:T(8,128)(2,1)S(1)}) custom-call(bf16[2,2,1024,512]{3,2,1,0:T(8,128)(2,1)} %x_hbm.7, bf16[2,2,256,1024]{3,2,1,0:T(8,128)(2,1)} %l_hbm.7, bf16[4,2,2,2,256,256]{5,4,3,2,1,0:T(8,128)(2,1)} %t_ref.23), custom_call_target="tpu_custom_call" | custom-call | flops 2 | bytes 2 | tf_op jit(solution)/shard_map/leaf/pallas_call | solution.py:143
  3.8 7.8 %collective-permute-start.9 = (bf16[2,2,256,128]{3,2,1,0:T(8,128)(2,1)S(1)}, bf16[2,2,256,128]{3,2,1,0:T(8,128)(2,1)S(1)}, u32[]{:S(2)}, u32[]{:S(2)}) collective-permute-start(bf16[2,2,256,128]{3,2,1,0:T(8,128)(2,1)S(1)} %get-tuple-element.48), channel_id=1, source_target_pairs={{0,128},{128,0},{8,136},{136,8},{16,144},{144,16},{24,152},{152,24... | collective-permute-start | bytes 786440 | tf_op jit(solution)/shard_map/ppermute | solution.py:22
  11.7 3.8 %leaf.6 = (bf16[2,2,256,128]{3,2,1,0:T(8,128)(2,1)S(1)}, bf16[2,2,256,128]{3,2,1,0:T(8,128)(2,1)S(1)}) custom-call(bf16[2,2,1024,512]{3,2,1,0:T(8,128)(2,1)} %x_hbm.7, bf16[2,2,256,1024]{3,2,1,0:T(8,128)(2,1)} %l_hbm.7, bf16[4,2,2,2,256,256]{5,4,3,2,1,0:T(8,128)(2,1)} %t_ref.23), custom_call_target="tpu_custom_call" | custom-call | flops 2 | bytes 2 | tf_op jit(solution)/shard_map/leaf/pallas_call | solution.py:143
  15.5 0.1 collective-permute-start.6
  15.6 3.8 %leaf.5 = (bf16[2,2,256,128]{3,2,1,0:T(8,128)(2,1)S(1)}, bf16[2,2,256,128]{3,2,1,0:T(8,128)(2,1)S(1)}) custom-call(bf16[2,2,1024,512]{3,2,1,0:T(8,128)(2,1)} %x_hbm.7, bf16[2,2,256,1024]{3,2,1,0:T(8,128)(2,1)} %l_hbm.7, bf16[4,2,2,2,256,256]{5,4,3,2,1,0:T(8,128)(2,1)} %t_ref.23), custom_call_target="tpu_custom_call" | custom-call | flops 2 | bytes 2 | tf_op jit(solution)/shard_map/leaf/pallas_call | solution.py:143
  19.5 0.0 copy-start
  19.5 5.4 %collective-permute-start.3 = (bf16[2,2,256,128]{3,2,1,0:T(8,128)(2,1)S(1)}, bf16[2,2,256,128]{3,2,1,0:T(8,128)(2,1)S(1)}, u32[]{:S(2)}, u32[]{:S(2)}) collective-permute-start(bf16[2,2,256,128]{3,2,1,0:T(8,128)(2,1)S(1)} %get-tuple-element.36), channel_id=1, source_target_pairs={{0,128},{128,0},{8,136},{136,8},{16,144},{144,16},{24,152},{152,24... | collective-permute-start | bytes 786440 | tf_op jit(solution)/shard_map/ppermute | solution.py:22
  24.9 3.8 %leaf.4 = (bf16[2,2,256,128]{3,2,1,0:T(8,128)(2,1)S(1)}, bf16[2,2,256,128]{3,2,1,0:T(8,128)(2,1)S(1)}) custom-call(bf16[2,2,1024,512]{3,2,1,0:T(8,128)(2,1)} %x_hbm.7, bf16[2,2,256,1024]{3,2,1,0:T(8,128)(2,1)} %l_hbm.7, bf16[4,2,2,2,256,256]{5,4,3,2,1,0:T(8,128)(2,1)} %t_ref.23), custom_call_target="tpu_custom_call" | custom-call | flops 2 | bytes 2 | tf_op jit(solution)/shard_map/leaf/pallas_call | solution.py:143
  28.7 0.2 collective-permute-start
  29.0 0.0 collective-permute-done.9.in_ref
  29.0 0.0 copy-done
  29.0 0.7 middle.14
  29.7 1.6 %collective-permute-start.10 = (bf16[2,2,256,128]{3,2,1,0:T(8,128)(2,1)S(1)}, bf16[2,2,256,128]{3,2,1,0:T(8,128)(2,1)S(1)}, u32[]{:S(2)}, u32[]{:S(2)}) collective-permute-start(bf16[2,2,256,128]{3,2,1,0:T(8,128)(2,1)S(1)} %get-tuple-element.50), channel_id=1, source_target_pairs={{0,64},{64,0},{8,72},{72,8},{16,80},{80,16},{24,88},{88,24},{32,96... | collective-permute-start | bytes 786440 | tf_op jit(solution)/shard_map/ppermute | solution.py:22
  31.2 8.3 %collective-permute-done.6.in_ref = bf16[2,2,256,128]{3,2,1,0:T(8,128)(2,1)S(1)} collective-permute-done((bf16[2,2,256,128]{3,2,1,0:T(8,128)(2,1)S(1)}, bf16[2,2,256,128]{3,2,1,0:T(8,128)(2,1)S(1)}, u32[]{:S(2)}, u32[]{:S(2)}) %collective-permute-start.6) | collective-permute-done | bytes 262176 | tf_op jit(solution)/shard_map/ppermute | solution.py:22
  39.6 0.7 middle.12
  40.3 0.1 collective-permute-start.7
  40.4 14.3 %collective-permute-done.3.in_ref = bf16[2,2,256,128]{3,2,1,0:T(8,128)(2,1)S(1)} collective-permute-done((bf16[2,2,256,128]{3,2,1,0:T(8,128)(2,1)S(1)}, bf16[2,2,256,128]{3,2,1,0:T(8,128)(2,1)S(1)}, u32[]{:S(2)}, u32[]{:S(2)}) %collective-permute-start.3) | collective-permute-done | bytes 262176 | tf_op jit(solution)/shard_map/ppermute | solution.py:22
  54.7 0.7 middle.10
  55.4 0.1 collective-permute-start.4
  55.5 4.8 %collective-permute-done.in_ref = bf16[2,2,256,128]{3,2,1,0:T(8,128)(2,1)S(1)} collective-permute-done((bf16[2,2,256,128]{3,2,1,0:T(8,128)(2,1)S(1)}, bf16[2,2,256,128]{3,2,1,0:T(8,128)(2,1)S(1)}, u32[]{:S(2)}, u32[]{:S(2)}) %collective-permute-start) | collective-permute-done | bytes 262176 | tf_op jit(solution)/shard_map/ppermute | solution.py:22
  60.3 0.7 middle.8
  61.0 0.3 collective-permute-start.1
  61.3 25.2 %collective-permute-done.10.in_ref = bf16[2,2,256,128]{3,2,1,0:T(8,128)(2,1)S(1)} collective-permute-done((bf16[2,2,256,128]{3,2,1,0:T(8,128)(2,1)S(1)}, bf16[2,2,256,128]{3,2,1,0:T(8,128)(2,1)S(1)}, u32[]{:S(2)}, u32[]{:S(2)}) %collective-permute-start.10) | collective-permute-done | bytes 262176 | tf_op jit(solution)/shard_map/ppermute | solution.py:22
  86.5 0.7 middle.15
  87.2 3.1 %collective-permute-start.11 = (bf16[2,2,256,128]{3,2,1,0:T(8,128)(2,1)S(1)}, bf16[2,2,256,128]{3,2,1,0:T(8,128)(2,1)S(1)}, u32[]{:S(2)}, u32[]{:S(2)}) collective-permute-start(bf16[2,2,256,128]{3,2,1,0:T(8,128)(2,1)S(1)} %get-tuple-element.52), channel_id=1, source_target_pairs={{0,4},{4,0},{1,5},{5,1},{2,6},{6,2},{3,7},{7,3},{8,12},{12,8},{9,1... | collective-permute-start | bytes 786440 | tf_op jit(solution)/shard_map/ppermute | solution.py:22
  90.3 1.9 %collective-permute-done.7.in_ref = bf16[2,2,256,128]{3,2,1,0:T(8,128)(2,1)S(1)} collective-permute-done((bf16[2,2,256,128]{3,2,1,0:T(8,128)(2,1)S(1)}, bf16[2,2,256,128]{3,2,1,0:T(8,128)(2,1)S(1)}, u32[]{:S(2)}, u32[]{:S(2)}) %collective-permute-start.7) | collective-permute-done | bytes 262176 | tf_op jit(solution)/shard_map/ppermute | solution.py:22
  92.1 0.7 middle.13
  92.8 3.1 %collective-permute-start.8 = (bf16[2,2,256,128]{3,2,1,0:T(8,128)(2,1)S(1)}, bf16[2,2,256,128]{3,2,1,0:T(8,128)(2,1)S(1)}, u32[]{:S(2)}, u32[]{:S(2)}) collective-permute-start(bf16[2,2,256,128]{3,2,1,0:T(8,128)(2,1)S(1)} %get-tuple-element.46), channel_id=1, source_target_pairs={{0,4},{4,0},{1,5},{5,1},{2,6},{6,2},{3,7},{7,3},{8,12},{12,8},{9,1... | collective-permute-start | bytes 786440 | tf_op jit(solution)/shard_map/ppermute | solution.py:22
  95.9 1.9 %collective-permute-done.4.in_ref = bf16[2,2,256,128]{3,2,1,0:T(8,128)(2,1)S(1)} collective-permute-done((bf16[2,2,256,128]{3,2,1,0:T(8,128)(2,1)S(1)}, bf16[2,2,256,128]{3,2,1,0:T(8,128)(2,1)S(1)}, u32[]{:S(2)}, u32[]{:S(2)}) %collective-permute-start.4) | collective-permute-done | bytes 262176 | tf_op jit(solution)/shard_map/ppermute | solution.py:22
  97.8 0.7 middle.11
  98.4 3.1 %collective-permute-start.5 = (bf16[2,2,256,128]{3,2,1,0:T(8,128)(2,1)S(1)}, bf16[2,2,256,128]{3,2,1,0:T(8,128)(2,1)S(1)}, u32[]{:S(2)}, u32[]{:S(2)}) collective-permute-start(bf16[2,2,256,128]{3,2,1,0:T(8,128)(2,1)S(1)} %get-tuple-element.40), channel_id=1, source_target_pairs={{0,4},{4,0},{1,5},{5,1},{2,6},{6,2},{3,7},{7,3},{8,12},{12,8},{9,1... | collective-permute-start | bytes 786440 | tf_op jit(solution)/shard_map/ppermute | solution.py:22
  101.5 1.9 %collective-permute-done.1.in_ref = bf16[2,2,256,128]{3,2,1,0:T(8,128)(2,1)S(1)} collective-permute-done((bf16[2,2,256,128]{3,2,1,0:T(8,128)(2,1)S(1)}, bf16[2,2,256,128]{3,2,1,0:T(8,128)(2,1)S(1)}, u32[]{:S(2)}, u32[]{:S(2)}) %collective-permute-start.1) | collective-permute-done | bytes 262176 | tf_op jit(solution)/shard_map/ppermute | solution.py:22
  103.4 0.7 middle.9
  104.1 3.1 %collective-permute-start.2 = (bf16[2,2,256,128]{3,2,1,0:T(8,128)(2,1)S(1)}, bf16[2,2,256,128]{3,2,1,0:T(8,128)(2,1)S(1)}, u32[]{:S(2)}, u32[]{:S(2)}) collective-permute-start(bf16[2,2,256,128]{3,2,1,0:T(8,128)(2,1)S(1)} %get-tuple-element.34), channel_id=1, source_target_pairs={{0,4},{4,0},{1,5},{5,1},{2,6},{6,2},{3,7},{7,3},{8,12},{12,8},{9,1... | collective-permute-start | bytes 786440 | tf_op jit(solution)/shard_map/ppermute | solution.py:22
  107.1 0.0 collective-permute-done.11.in_ref
  107.1 1.0 last.4.refs_0_
  108.2 0.0 collective-permute-done.8.in_ref
  108.2 1.0 last.5.refs_0_
  109.2 0.0 collective-permute-done.5.in_ref
  109.2 1.0 last.6.refs_0_
  110.2 2.8 %collective-permute-done.2.in_ref = bf16[2,2,256,128]{3,2,1,0:T(8,128)(2,1)S(1)} collective-permute-done((bf16[2,2,256,128]{3,2,1,0:T(8,128)(2,1)S(1)}, bf16[2,2,256,128]{3,2,1,0:T(8,128)(2,1)S(1)}, u32[]{:S(2)}, u32[]{:S(2)}) %collective-permute-start.2) | collective-permute-done | bytes 262176 | tf_op jit(solution)/shard_map/ppermute | solution.py:22
  113.1 1.0 last.7
Async XLA Ops:
  3.8 25.2 %collective-permute-start.9 = (bf16[2,2,256,128]{3,2,1,0:T(8,128)(2,1)S(1)}, bf16[2,2,256,128]{3,2,1,0:T(8,128)(2,1)S(1)}, u32[]{:S(2)}, u32[]{:S(2)}) collective-permute-start(bf16[2,2,256,128]{3,2,1,0:T(8,128)(2,1)S(1)} %get-tuple-element.48), channel_id=1, source_target_pairs={{0,128},{128,0},{8,136},{136,8},{16,144},{144,16},{24,152},{152,24... | collective-permute-start | bytes 786440 | tf_op jit(solution)/shard_map/ppermute | solution.py:22
  15.5 24.1 %collective-permute-start.6 = (bf16[2,2,256,128]{3,2,1,0:T(8,128)(2,1)S(1)}, bf16[2,2,256,128]{3,2,1,0:T(8,128)(2,1)S(1)}, u32[]{:S(2)}, u32[]{:S(2)}) collective-permute-start(bf16[2,2,256,128]{3,2,1,0:T(8,128)(2,1)S(1)} %get-tuple-element.42), channel_id=1, source_target_pairs={{0,128},{128,0},{8,136},{136,8},{16,144},{144,16},{24,152},{152,24... | collective-permute-start | bytes 786440 | tf_op jit(solution)/shard_map/ppermute | solution.py:22
  19.5 9.5 %copy-start = (bf16[4,2,2,2,256,256]{5,4,3,2,1,0:T(8,128)(2,1)S(1)}, bf16[4,2,2,2,256,256]{5,4,3,2,1,0:T(8,128)(2,1)}, u32[]{:S(2)}) copy-start(bf16[4,2,2,2,256,256]{5,4,3,2,1,0:T(8,128)(2,1)} %t_ref.23) | copy-start | bytes 12582916
  19.5 35.2 %collective-permute-start.3 = (bf16[2,2,256,128]{3,2,1,0:T(8,128)(2,1)S(1)}, bf16[2,2,256,128]{3,2,1,0:T(8,128)(2,1)S(1)}, u32[]{:S(2)}, u32[]{:S(2)}) collective-permute-start(bf16[2,2,256,128]{3,2,1,0:T(8,128)(2,1)S(1)} %get-tuple-element.36), channel_id=1, source_target_pairs={{0,128},{128,0},{8,136},{136,8},{16,144},{144,16},{24,152},{152,24... | collective-permute-start | bytes 786440 | tf_op jit(solution)/shard_map/ppermute | solution.py:22
  28.7 31.6 %collective-permute-start = (bf16[2,2,256,128]{3,2,1,0:T(8,128)(2,1)S(1)}, bf16[2,2,256,128]{3,2,1,0:T(8,128)(2,1)S(1)}, u32[]{:S(2)}, u32[]{:S(2)}) collective-permute-start(bf16[2,2,256,128]{3,2,1,0:T(8,128)(2,1)S(1)} %get-tuple-element.30), channel_id=1, source_target_pairs={{0,128},{128,0},{8,136},{136,8},{16,144},{144,16},{24,152},{152,24... | collective-permute-start | bytes 786440 | tf_op jit(solution)/shard_map/ppermute | solution.py:22
  29.7 56.8 %collective-permute-start.10 = (bf16[2,2,256,128]{3,2,1,0:T(8,128)(2,1)S(1)}, bf16[2,2,256,128]{3,2,1,0:T(8,128)(2,1)S(1)}, u32[]{:S(2)}, u32[]{:S(2)}) collective-permute-start(bf16[2,2,256,128]{3,2,1,0:T(8,128)(2,1)S(1)} %get-tuple-element.50), channel_id=1, source_target_pairs={{0,64},{64,0},{8,72},{72,8},{16,80},{80,16},{24,88},{88,24},{32,96... | collective-permute-start | bytes 786440 | tf_op jit(solution)/shard_map/ppermute | solution.py:22
  40.3 51.9 %collective-permute-start.7 = (bf16[2,2,256,128]{3,2,1,0:T(8,128)(2,1)S(1)}, bf16[2,2,256,128]{3,2,1,0:T(8,128)(2,1)S(1)}, u32[]{:S(2)}, u32[]{:S(2)}) collective-permute-start(bf16[2,2,256,128]{3,2,1,0:T(8,128)(2,1)S(1)} %get-tuple-element.44), channel_id=1, source_target_pairs={{0,64},{64,0},{8,72},{72,8},{16,80},{80,16},{24,88},{88,24},{32,96... | collective-permute-start | bytes 786440 | tf_op jit(solution)/shard_map/ppermute | solution.py:22
  55.4 42.4 %collective-permute-start.4 = (bf16[2,2,256,128]{3,2,1,0:T(8,128)(2,1)S(1)}, bf16[2,2,256,128]{3,2,1,0:T(8,128)(2,1)S(1)}, u32[]{:S(2)}, u32[]{:S(2)}) collective-permute-start(bf16[2,2,256,128]{3,2,1,0:T(8,128)(2,1)S(1)} %get-tuple-element.38), channel_id=1, source_target_pairs={{0,64},{64,0},{8,72},{72,8},{16,80},{80,16},{24,88},{88,24},{32,96... | collective-permute-start | bytes 786440 | tf_op jit(solution)/shard_map/ppermute | solution.py:22
  61.0 42.4 %collective-permute-start.1 = (bf16[2,2,256,128]{3,2,1,0:T(8,128)(2,1)S(1)}, bf16[2,2,256,128]{3,2,1,0:T(8,128)(2,1)S(1)}, u32[]{:S(2)}, u32[]{:S(2)}) collective-permute-start(bf16[2,2,256,128]{3,2,1,0:T(8,128)(2,1)S(1)} %get-tuple-element.32), channel_id=1, source_target_pairs={{0,64},{64,0},{8,72},{72,8},{16,80},{80,16},{24,88},{88,24},{32,96... | collective-permute-start | bytes 786440 | tf_op jit(solution)/shard_map/ppermute | solution.py:22
  87.2 19.9 %collective-permute-start.11 = (bf16[2,2,256,128]{3,2,1,0:T(8,128)(2,1)S(1)}, bf16[2,2,256,128]{3,2,1,0:T(8,128)(2,1)S(1)}, u32[]{:S(2)}, u32[]{:S(2)}) collective-permute-start(bf16[2,2,256,128]{3,2,1,0:T(8,128)(2,1)S(1)} %get-tuple-element.52), channel_id=1, source_target_pairs={{0,4},{4,0},{1,5},{5,1},{2,6},{6,2},{3,7},{7,3},{8,12},{12,8},{9,1... | collective-permute-start | bytes 786440 | tf_op jit(solution)/shard_map/ppermute | solution.py:22
  92.8 15.3 %collective-permute-start.8 = (bf16[2,2,256,128]{3,2,1,0:T(8,128)(2,1)S(1)}, bf16[2,2,256,128]{3,2,1,0:T(8,128)(2,1)S(1)}, u32[]{:S(2)}, u32[]{:S(2)}) collective-permute-start(bf16[2,2,256,128]{3,2,1,0:T(8,128)(2,1)S(1)} %get-tuple-element.46), channel_id=1, source_target_pairs={{0,4},{4,0},{1,5},{5,1},{2,6},{6,2},{3,7},{7,3},{8,12},{12,8},{9,1... | collective-permute-start | bytes 786440 | tf_op jit(solution)/shard_map/ppermute | solution.py:22
  98.4 10.8 %collective-permute-start.5 = (bf16[2,2,256,128]{3,2,1,0:T(8,128)(2,1)S(1)}, bf16[2,2,256,128]{3,2,1,0:T(8,128)(2,1)S(1)}, u32[]{:S(2)}, u32[]{:S(2)}) collective-permute-start(bf16[2,2,256,128]{3,2,1,0:T(8,128)(2,1)S(1)} %get-tuple-element.40), channel_id=1, source_target_pairs={{0,4},{4,0},{1,5},{5,1},{2,6},{6,2},{3,7},{7,3},{8,12},{12,8},{9,1... | collective-permute-start | bytes 786440 | tf_op jit(solution)/shard_map/ppermute | solution.py:22
  104.1 9.0 %collective-permute-start.2 = (bf16[2,2,256,128]{3,2,1,0:T(8,128)(2,1)S(1)}, bf16[2,2,256,128]{3,2,1,0:T(8,128)(2,1)S(1)}, u32[]{:S(2)}, u32[]{:S(2)}) collective-permute-start(bf16[2,2,256,128]{3,2,1,0:T(8,128)(2,1)S(1)} %get-tuple-element.34), channel_id=1, source_target_pairs={{0,4},{4,0},{1,5},{5,1},{2,6},{6,2},{3,7},{7,3},{8,12},{12,8},{9,1... | collective-permute-start | bytes 786440 | tf_op jit(solution)/shard_map/ppermute | solution.py:22

commit v4 on v3

--- a/solution.py
+++ b/solution.py
@@ -83,11 +83,22 @@
         p_refs[b][...] = product(t1[b], after).astype(jnp.bfloat16)
 
 
+def own_kernel(level, nodes, place, a_ref, t_ref, own_ref):
+    own = own_bit(*place)
+    for at, node in enumerate(nodes):
+        own_ref[at] = product(t_ref[level, node, own], a_ref[at])
+
+
+def own_term_of(held, t_ref, level, at, node, place):
+    if held.dtype == jnp.float32:
+        return held[at]
+    return product(t_ref[level, node, own_bit(*place)], held[at])
+
+
 def middle_kernel(level, nodes, place, next_place, a_ref, in_ref, t_ref, a_out, p_out):
-    own = own_bit(*place)
     other = 1 - own_bit(*next_place)
     for at, node in enumerate(nodes):
-        own_term = product(t_ref[level, node, own], a_ref[at])
+        own_term = own_term_of(a_ref, t_ref, level, at, node, place)
         after = (own_term + in_ref[at].astype(jnp.float32)).astype(jnp.bfloat16)
         a_out[at] = after
         p_out[at] = product(t_ref[level + 1, node, other], after).astype(jnp.bfloat16)
@@ -95,10 +106,9 @@
 
 def last_kernel(level, nodes, start, width, place, a_ref, in_ref, t_ref, *refs):
     out_hbm, out, sems = refs[-3:]
-    own = own_bit(*place)
     stores = []
     for at, node in enumerate(nodes):
-        own_term = product(t_ref[level, node, own], a_ref[at])
+        own_term = own_term_of(a_ref, t_ref, level, at, node, place)
         out[at] = (own_term + in_ref[at].astype(jnp.float32)).astype(jnp.bfloat16)
         stores.append(
             pltpu.make_async_copy(
@@ -157,6 +167,18 @@
             name="leaf",
         )(*in_hbm)
 
+    def own(level, chunk, held):
+        group, some = chunk
+        return pl.pallas_call(
+            functools.partial(own_kernel, level, some, places[level]),
+            out_shape=jax.ShapeDtypeStruct((len(some), 2, rank, widths[group]), jnp.float32),
+            in_specs=[here] * 2,
+            out_specs=here,
+            compiler_params=params(LIMIT),
+            cost_estimate=cost,
+            name="own",
+        )(held, transfer_blocks)
+
     def middle(level, chunk, held, arrived):
         group, some = chunk
         return pl.pallas_call(
@@ -204,6 +226,7 @@
         for chunk in chunks:
             held[chunk], term = middle(level, chunk, held[chunk], flying[chunk])
             flying[chunk] = partner_2(term, *places[level + 1])
+            held[chunk] = own(level + 1, chunk, held[chunk])
     result = None
     for chunk in chunks:
         result = last(3, chunk, held[chunk], flying[chunk], result)

time: 114 us -> 114 us (level)
    pallas_call x0 -> x8, Pallas kernels: none -> 2.36 us  [own(): pl.pallas_call(functools.partial(own_kernel, level, some, places[level]),...]
    pallas_call x8, Pallas kernels: 5.38 us -> 3.91 us  [middle(): pl.pallas_call(functools.partial(middle_kernel, level, some, places[level...]
  transfers between devices with their start and end apart: 12 -> 12, of which waited for: 8 -> 8; matrix products, arithmetic and copies ran while one was open for 0% -> 0% of each run, Pallas kernels for 17% -> 18%
where the time goes in v4:
time: 114 us
  waiting for transfers between devices  60.7 us (53%)
  starting transfers between devices  27.9 us (24%)
  Pallas kernels  24.6 us (22%)
    ppermute x12, waiting for transfers between devices, partner_2(): return lax.ppermute(block, axis, route)  60.7 us
    ppermute x12, starting transfers between devices, partner_2(): return lax.ppermute(block, axis, route)  27.9 us
    pallas_call x4, Pallas kernels, leaf(): pl.pallas_call(functools.partial(leaf_kernel, starts[group], width, apart...  15.3 us
    pallas_call x8, Pallas kernels, middle(): pl.pallas_call(functools.partial(middle_kernel, level, some, places[level...  3.91 us
    pallas_call x4, Pallas kernels, last(): pl.pallas_call(functools.partial(last_kernel, level, some, starts[group],...  2.97 us
    pallas_call x8, Pallas kernels, own(): pl.pallas_call(functools.partial(own_kernel, level, some, places[level]),...  2.36 us
  transfers between devices with their start and end apart: 12, of which 8 were waited for; matrix products, arithmetic and copies ran while one was open for 0% of the time, Pallas kernels for 18%

profile of v4, /device:TPU:1, one launch (start us, length us, event | category | flops | bytes accessed | tf_op | source)
XLA Modules:
  0.0 113.6 jit_solution(13907656746919331989)
XLA Ops:
  0.0 3.8 %leaf.7 = (bf16[2,2,256,128]{3,2,1,0:T(8,128)(2,1)S(1)}, bf16[2,2,256,128]{3,2,1,0:T(8,128)(2,1)S(1)}) custom-call(bf16[2,2,1024,512]{3,2,1,0:T(8,128)(2,1)} %x_hbm.7, bf16[2,2,256,1024]{3,2,1,0:T(8,128)(2,1)} %l_hbm.7, bf16[4,2,2,2,256,256]{5,4,3,2,1,0:T(8,128)(2,1)} %t_ref.39), custom_call_target="tpu_custom_call" | custom-call | flops 2 | bytes 2 | tf_op jit(solution)/shard_map/leaf/pallas_call | solution.py:153
  3.8 7.8 %collective-permute-start.9 = (bf16[2,2,256,128]{3,2,1,0:T(8,128)(2,1)S(1)}, bf16[2,2,256,128]{3,2,1,0:T(8,128)(2,1)S(1)}, u32[]{:S(2)}, u32[]{:S(2)}) collective-permute-start(bf16[2,2,256,128]{3,2,1,0:T(8,128)(2,1)S(1)} %get-tuple-element.48), channel_id=1, source_target_pairs={{0,128},{128,0},{8,136},{136,8},{16,144},{144,16},{24,152},{152,24... | collective-permute-start | bytes 786440 | tf_op jit(solution)/shard_map/ppermute | solution.py:22
  11.7 3.8 %leaf.6 = (bf16[2,2,256,128]{3,2,1,0:T(8,128)(2,1)S(1)}, bf16[2,2,256,128]{3,2,1,0:T(8,128)(2,1)S(1)}) custom-call(bf16[2,2,1024,512]{3,2,1,0:T(8,128)(2,1)} %x_hbm.7, bf16[2,2,256,1024]{3,2,1,0:T(8,128)(2,1)} %l_hbm.7, bf16[4,2,2,2,256,256]{5,4,3,2,1,0:T(8,128)(2,1)} %t_ref.39), custom_call_target="tpu_custom_call" | custom-call | flops 2 | bytes 2 | tf_op jit(solution)/shard_map/leaf/pallas_call | solution.py:153
  15.5 0.1 collective-permute-start.6
  15.6 3.8 %leaf.5 = (bf16[2,2,256,128]{3,2,1,0:T(8,128)(2,1)S(1)}, bf16[2,2,256,128]{3,2,1,0:T(8,128)(2,1)S(1)}) custom-call(bf16[2,2,1024,512]{3,2,1,0:T(8,128)(2,1)} %x_hbm.7, bf16[2,2,256,1024]{3,2,1,0:T(8,128)(2,1)} %l_hbm.7, bf16[4,2,2,2,256,256]{5,4,3,2,1,0:T(8,128)(2,1)} %t_ref.39), custom_call_target="tpu_custom_call" | custom-call | flops 2 | bytes 2 | tf_op jit(solution)/shard_map/leaf/pallas_call | solution.py:153
  19.5 0.0 copy-start
  19.5 5.4 %collective-permute-start.3 = (bf16[2,2,256,128]{3,2,1,0:T(8,128)(2,1)S(1)}, bf16[2,2,256,128]{3,2,1,0:T(8,128)(2,1)S(1)}, u32[]{:S(2)}, u32[]{:S(2)}) collective-permute-start(bf16[2,2,256,128]{3,2,1,0:T(8,128)(2,1)S(1)} %get-tuple-element.36), channel_id=1, source_target_pairs={{0,128},{128,0},{8,136},{136,8},{16,144},{144,16},{24,152},{152,24... | collective-permute-start | bytes 786440 | tf_op jit(solution)/shard_map/ppermute | solution.py:22
  24.9 3.8 %leaf.4 = (bf16[2,2,256,128]{3,2,1,0:T(8,128)(2,1)S(1)}, bf16[2,2,256,128]{3,2,1,0:T(8,128)(2,1)S(1)}) custom-call(bf16[2,2,1024,512]{3,2,1,0:T(8,128)(2,1)} %x_hbm.7, bf16[2,2,256,1024]{3,2,1,0:T(8,128)(2,1)} %l_hbm.7, bf16[4,2,2,2,256,256]{5,4,3,2,1,0:T(8,128)(2,1)} %t_ref.39), custom_call_target="tpu_custom_call" | custom-call | flops 2 | bytes 2 | tf_op jit(solution)/shard_map/leaf/pallas_call | solution.py:153
  28.7 0.2 collective-permute-start
  29.0 0.0 collective-permute-done.9.in_ref
  29.0 0.7 middle.14
  29.7 1.6 %collective-permute-start.10 = (bf16[2,2,256,128]{3,2,1,0:T(8,128)(2,1)S(1)}, bf16[2,2,256,128]{3,2,1,0:T(8,128)(2,1)S(1)}, u32[]{:S(2)}, u32[]{:S(2)}) collective-permute-start(bf16[2,2,256,128]{3,2,1,0:T(8,128)(2,1)S(1)} %get-tuple-element.50), channel_id=1, source_target_pairs={{0,64},{64,0},{8,72},{72,8},{16,80},{80,16},{24,88},{88,24},{32,96... | collective-permute-start | bytes 786440 | tf_op jit(solution)/shard_map/ppermute | solution.py:22
  31.2 8.3 %collective-permute-done.6.in_ref = bf16[2,2,256,128]{3,2,1,0:T(8,128)(2,1)S(1)} collective-permute-done((bf16[2,2,256,128]{3,2,1,0:T(8,128)(2,1)S(1)}, bf16[2,2,256,128]{3,2,1,0:T(8,128)(2,1)S(1)}, u32[]{:S(2)}, u32[]{:S(2)}) %collective-permute-start.6) | collective-permute-done | bytes 262176 | tf_op jit(solution)/shard_map/ppermute | solution.py:22
  39.6 0.7 middle.12
  40.3 0.1 collective-permute-start.7
  40.4 14.3 %collective-permute-done.3.in_ref = bf16[2,2,256,128]{3,2,1,0:T(8,128)(2,1)S(1)} collective-permute-done((bf16[2,2,256,128]{3,2,1,0:T(8,128)(2,1)S(1)}, bf16[2,2,256,128]{3,2,1,0:T(8,128)(2,1)S(1)}, u32[]{:S(2)}, u32[]{:S(2)}) %collective-permute-start.3) | collective-permute-done | bytes 262176 | tf_op jit(solution)/shard_map/ppermute | solution.py:22
  54.7 0.7 middle.10
  55.4 0.1 collective-permute-start.4
  55.5 4.8 %collective-permute-done.in_ref = bf16[2,2,256,128]{3,2,1,0:T(8,128)(2,1)S(1)} collective-permute-done((bf16[2,2,256,128]{3,2,1,0:T(8,128)(2,1)S(1)}, bf16[2,2,256,128]{3,2,1,0:T(8,128)(2,1)S(1)}, u32[]{:S(2)}, u32[]{:S(2)}) %collective-permute-start) | collective-permute-done | bytes 262176 | tf_op jit(solution)/shard_map/ppermute | solution.py:22
  60.3 0.7 middle.8
  61.0 0.3 collective-permute-start.1
  61.3 0.3 own.14.a_ref
  61.6 0.3 own.12.a_ref
  61.9 0.3 own.10.a_ref
  62.2 0.3 own.8.a_ref
  62.5 24.0 %collective-permute-done.10.in_ref = bf16[2,2,256,128]{3,2,1,0:T(8,128)(2,1)S(1)} collective-permute-done((bf16[2,2,256,128]{3,2,1,0:T(8,128)(2,1)S(1)}, bf16[2,2,256,128]{3,2,1,0:T(8,128)(2,1)S(1)}, u32[]{:S(2)}, u32[]{:S(2)}) %collective-permute-start.10) | collective-permute-done | bytes 262176 | tf_op jit(solution)/shard_map/ppermute | solution.py:22
  86.5 0.3 middle.15
  86.8 3.1 %collective-permute-start.11 = (bf16[2,2,256,128]{3,2,1,0:T(8,128)(2,1)S(1)}, bf16[2,2,256,128]{3,2,1,0:T(8,128)(2,1)S(1)}, u32[]{:S(2)}, u32[]{:S(2)}) collective-permute-start(bf16[2,2,256,128]{3,2,1,0:T(8,128)(2,1)S(1)} %get-tuple-element.52), channel_id=1, source_target_pairs={{0,4},{4,0},{1,5},{5,1},{2,6},{6,2},{3,7},{7,3},{8,12},{12,8},{9,1... | collective-permute-start | bytes 786440 | tf_op jit(solution)/shard_map/ppermute | solution.py:22
  89.9 2.2 %collective-permute-done.7.in_ref = bf16[2,2,256,128]{3,2,1,0:T(8,128)(2,1)S(1)} collective-permute-done((bf16[2,2,256,128]{3,2,1,0:T(8,128)(2,1)S(1)}, bf16[2,2,256,128]{3,2,1,0:T(8,128)(2,1)S(1)}, u32[]{:S(2)}, u32[]{:S(2)}) %collective-permute-start.7) | collective-permute-done | bytes 262176 | tf_op jit(solution)/shard_map/ppermute | solution.py:22
  92.1 0.3 middle.13
  92.5 3.1 %collective-permute-start.8 = (bf16[2,2,256,128]{3,2,1,0:T(8,128)(2,1)S(1)}, bf16[2,2,256,128]{3,2,1,0:T(8,128)(2,1)S(1)}, u32[]{:S(2)}, u32[]{:S(2)}) collective-permute-start(bf16[2,2,256,128]{3,2,1,0:T(8,128)(2,1)S(1)} %get-tuple-element.46), channel_id=1, source_target_pairs={{0,4},{4,0},{1,5},{5,1},{2,6},{6,2},{3,7},{7,3},{8,12},{12,8},{9,1... | collective-permute-start | bytes 786440 | tf_op jit(solution)/shard_map/ppermute | solution.py:22
  95.5 2.2 %collective-permute-done.4.in_ref = bf16[2,2,256,128]{3,2,1,0:T(8,128)(2,1)S(1)} collective-permute-done((bf16[2,2,256,128]{3,2,1,0:T(8,128)(2,1)S(1)}, bf16[2,2,256,128]{3,2,1,0:T(8,128)(2,1)S(1)}, u32[]{:S(2)}, u32[]{:S(2)}) %collective-permute-start.4) | collective-permute-done | bytes 262176 | tf_op jit(solution)/shard_map/ppermute | solution.py:22
  97.8 0.3 middle.11
  98.1 3.1 %collective-permute-start.5 = (bf16[2,2,256,128]{3,2,1,0:T(8,128)(2,1)S(1)}, bf16[2,2,256,128]{3,2,1,0:T(8,128)(2,1)S(1)}, u32[]{:S(2)}, u32[]{:S(2)}) collective-permute-start(bf16[2,2,256,128]{3,2,1,0:T(8,128)(2,1)S(1)} %get-tuple-element.40), channel_id=1, source_target_pairs={{0,4},{4,0},{1,5},{5,1},{2,6},{6,2},{3,7},{7,3},{8,12},{12,8},{9,1... | collective-permute-start | bytes 786440 | tf_op jit(solution)/shard_map/ppermute | solution.py:22
  101.1 2.2 %collective-permute-done.1.in_ref = bf16[2,2,256,128]{3,2,1,0:T(8,128)(2,1)S(1)} collective-permute-done((bf16[2,2,256,128]{3,2,1,0:T(8,128)(2,1)S(1)}, bf16[2,2,256,128]{3,2,1,0:T(8,128)(2,1)S(1)}, u32[]{:S(2)}, u32[]{:S(2)}) %collective-permute-start.1) | collective-permute-done | bytes 262176 | tf_op jit(solution)/shard_map/ppermute | solution.py:22
  103.4 0.3 middle.9
  103.7 3.1 %collective-permute-start.2 = (bf16[2,2,256,128]{3,2,1,0:T(8,128)(2,1)S(1)}, bf16[2,2,256,128]{3,2,1,0:T(8,128)(2,1)S(1)}, u32[]{:S(2)}, u32[]{:S(2)}) collective-permute-start(bf16[2,2,256,128]{3,2,1,0:T(8,128)(2,1)S(1)} %get-tuple-element.34), channel_id=1, source_target_pairs={{0,4},{4,0},{1,5},{5,1},{2,6},{6,2},{3,7},{7,3},{8,12},{12,8},{9,1... | collective-permute-start | bytes 786440 | tf_op jit(solution)/shard_map/ppermute | solution.py:22
  106.8 0.3 own.15.a_ref
  107.1 0.3 own.13.a_ref
  107.4 0.3 own.11.a_ref
  107.7 0.3 own.9.a_ref
  108.0 0.0 collective-permute-done.11.in_ref
  108.0 0.7 last.4.refs_0_
  108.7 0.7 last.5.refs_0_
  109.5 0.0 collective-permute-done.5.in_ref
  109.5 0.7 last.6.refs_0_
  110.3 2.4 %collective-permute-done.2.in_ref = bf16[2,2,256,128]{3,2,1,0:T(8,128)(2,1)S(1)} collective-permute-done((bf16[2,2,256,128]{3,2,1,0:T(8,128)(2,1)S(1)}, bf16[2,2,256,128]{3,2,1,0:T(8,128)(2,1)S(1)}, u32[]{:S(2)}, u32[]{:S(2)}) %collective-permute-start.2) | collective-permute-done | bytes 262176 | tf_op jit(solution)/shard_map/ppermute | solution.py:22
  112.7 0.7 last.7
  (2 shorter events, 0.0 us)
Async XLA Ops:
  3.8 25.2 %collective-permute-start.9 = (bf16[2,2,256,128]{3,2,1,0:T(8,128)(2,1)S(1)}, bf16[2,2,256,128]{3,2,1,0:T(8,128)(2,1)S(1)}, u32[]{:S(2)}, u32[]{:S(2)}) collective-permute-start(bf16[2,2,256,128]{3,2,1,0:T(8,128)(2,1)S(1)} %get-tuple-element.48), channel_id=1, source_target_pairs={{0,128},{128,0},{8,136},{136,8},{16,144},{144,16},{24,152},{152,24... | collective-permute-start | bytes 786440 | tf_op jit(solution)/shard_map/ppermute | solution.py:22
  15.5 24.1 %collective-permute-start.6 = (bf16[2,2,256,128]{3,2,1,0:T(8,128)(2,1)S(1)}, bf16[2,2,256,128]{3,2,1,0:T(8,128)(2,1)S(1)}, u32[]{:S(2)}, u32[]{:S(2)}) collective-permute-start(bf16[2,2,256,128]{3,2,1,0:T(8,128)(2,1)S(1)} %get-tuple-element.42), channel_id=1, source_target_pairs={{0,128},{128,0},{8,136},{136,8},{16,144},{144,16},{24,152},{152,24... | collective-permute-start | bytes 786440 | tf_op jit(solution)/shard_map/ppermute | solution.py:22
  19.5 9.5 %copy-start = (bf16[4,2,2,2,256,256]{5,4,3,2,1,0:T(8,128)(2,1)S(1)}, bf16[4,2,2,2,256,256]{5,4,3,2,1,0:T(8,128)(2,1)}, u32[]{:S(2)}) copy-start(bf16[4,2,2,2,256,256]{5,4,3,2,1,0:T(8,128)(2,1)} %t_ref.39) | copy-start | bytes 12582916
  19.5 35.2 %collective-permute-start.3 = (bf16[2,2,256,128]{3,2,1,0:T(8,128)(2,1)S(1)}, bf16[2,2,256,128]{3,2,1,0:T(8,128)(2,1)S(1)}, u32[]{:S(2)}, u32[]{:S(2)}) collective-permute-start(bf16[2,2,256,128]{3,2,1,0:T(8,128)(2,1)S(1)} %get-tuple-element.36), channel_id=1, source_target_pairs={{0,128},{128,0},{8,136},{136,8},{16,144},{144,16},{24,152},{152,24... | collective-permute-start | bytes 786440 | tf_op jit(solution)/shard_map/ppermute | solution.py:22
  28.7 31.6 %collective-permute-start = (bf16[2,2,256,128]{3,2,1,0:T(8,128)(2,1)S(1)}, bf16[2,2,256,128]{3,2,1,0:T(8,128)(2,1)S(1)}, u32[]{:S(2)}, u32[]{:S(2)}) collective-permute-start(bf16[2,2,256,128]{3,2,1,0:T(8,128)(2,1)S(1)} %get-tuple-element.30), channel_id=1, source_target_pairs={{0,128},{128,0},{8,136},{136,8},{16,144},{144,16},{24,152},{152,24... | collective-permute-start | bytes 786440 | tf_op jit(solution)/shard_map/ppermute | solution.py:22
  29.7 56.8 %collective-permute-start.10 = (bf16[2,2,256,128]{3,2,1,0:T(8,128)(2,1)S(1)}, bf16[2,2,256,128]{3,2,1,0:T(8,128)(2,1)S(1)}, u32[]{:S(2)}, u32[]{:S(2)}) collective-permute-start(bf16[2,2,256,128]{3,2,1,0:T(8,128)(2,1)S(1)} %get-tuple-element.50), channel_id=1, source_target_pairs={{0,64},{64,0},{8,72},{72,8},{16,80},{80,16},{24,88},{88,24},{32,96... | collective-permute-start | bytes 786440 | tf_op jit(solution)/shard_map/ppermute | solution.py:22
  40.3 51.9 %collective-permute-start.7 = (bf16[2,2,256,128]{3,2,1,0:T(8,128)(2,1)S(1)}, bf16[2,2,256,128]{3,2,1,0:T(8,128)(2,1)S(1)}, u32[]{:S(2)}, u32[]{:S(2)}) collective-permute-start(bf16[2,2,256,128]{3,2,1,0:T(8,128)(2,1)S(1)} %get-tuple-element.44), channel_id=1, source_target_pairs={{0,64},{64,0},{8,72},{72,8},{16,80},{80,16},{24,88},{88,24},{32,96... | collective-permute-start | bytes 786440 | tf_op jit(solution)/shard_map/ppermute | solution.py:22
  55.4 42.4 %collective-permute-start.4 = (bf16[2,2,256,128]{3,2,1,0:T(8,128)(2,1)S(1)}, bf16[2,2,256,128]{3,2,1,0:T(8,128)(2,1)S(1)}, u32[]{:S(2)}, u32[]{:S(2)}) collective-permute-start(bf16[2,2,256,128]{3,2,1,0:T(8,128)(2,1)S(1)} %get-tuple-element.38), channel_id=1, source_target_pairs={{0,64},{64,0},{8,72},{72,8},{16,80},{80,16},{24,88},{88,24},{32,96... | collective-permute-start | bytes 786440 | tf_op jit(solution)/shard_map/ppermute | solution.py:22
  61.0 42.4 %collective-permute-start.1 = (bf16[2,2,256,128]{3,2,1,0:T(8,128)(2,1)S(1)}, bf16[2,2,256,128]{3,2,1,0:T(8,128)(2,1)S(1)}, u32[]{:S(2)}, u32[]{:S(2)}) collective-permute-start(bf16[2,2,256,128]{3,2,1,0:T(8,128)(2,1)S(1)} %get-tuple-element.32), channel_id=1, source_target_pairs={{0,64},{64,0},{8,72},{72,8},{16,80},{80,16},{24,88},{88,24},{32,96... | collective-permute-start | bytes 786440 | tf_op jit(solution)/shard_map/ppermute | solution.py:22
  86.8 21.1 %collective-permute-start.11 = (bf16[2,2,256,128]{3,2,1,0:T(8,128)(2,1)S(1)}, bf16[2,2,256,128]{3,2,1,0:T(8,128)(2,1)S(1)}, u32[]{:S(2)}, u32[]{:S(2)}) collective-permute-start(bf16[2,2,256,128]{3,2,1,0:T(8,128)(2,1)S(1)} %get-tuple-element.52), channel_id=1, source_target_pairs={{0,4},{4,0},{1,5},{5,1},{2,6},{6,2},{3,7},{7,3},{8,12},{12,8},{9,1... | collective-permute-start | bytes 786440 | tf_op jit(solution)/shard_map/ppermute | solution.py:22
  92.5 16.3 %collective-permute-start.8 = (bf16[2,2,256,128]{3,2,1,0:T(8,128)(2,1)S(1)}, bf16[2,2,256,128]{3,2,1,0:T(8,128)(2,1)S(1)}, u32[]{:S(2)}, u32[]{:S(2)}) collective-permute-start(bf16[2,2,256,128]{3,2,1,0:T(8,128)(2,1)S(1)} %get-tuple-element.46), channel_id=1, source_target_pairs={{0,4},{4,0},{1,5},{5,1},{2,6},{6,2},{3,7},{7,3},{8,12},{12,8},{9,1... | collective-permute-start | bytes 786440 | tf_op jit(solution)/shard_map/ppermute | solution.py:22
  98.1 11.4 %collective-permute-start.5 = (bf16[2,2,256,128]{3,2,1,0:T(8,128)(2,1)S(1)}, bf16[2,2,256,128]{3,2,1,0:T(8,128)(2,1)S(1)}, u32[]{:S(2)}, u32[]{:S(2)}) collective-permute-start(bf16[2,2,256,128]{3,2,1,0:T(8,128)(2,1)S(1)} %get-tuple-element.40), channel_id=1, source_target_pairs={{0,4},{4,0},{1,5},{5,1},{2,6},{6,2},{3,7},{7,3},{8,12},{12,8},{9,1... | collective-permute-start | bytes 786440 | tf_op jit(solution)/shard_map/ppermute | solution.py:22
  103.7 9.0 %collective-permute-start.2 = (bf16[2,2,256,128]{3,2,1,0:T(8,128)(2,1)S(1)}, bf16[2,2,256,128]{3,2,1,0:T(8,128)(2,1)S(1)}, u32[]{:S(2)}, u32[]{:S(2)}) collective-permute-start(bf16[2,2,256,128]{3,2,1,0:T(8,128)(2,1)S(1)} %get-tuple-element.34), channel_id=1, source_target_pairs={{0,4},{4,0},{1,5},{5,1},{2,6},{6,2},{3,7},{7,3},{8,12},{12,8},{9,1... | collective-permute-start | bytes 786440 | tf_op jit(solution)/shard_map/ppermute | solution.py:22

commit v5 on v4

--- a/solution.py
+++ b/solution.py
@@ -7,7 +7,7 @@
 from jax.experimental.pallas import tpu as pltpu
 from jax.sharding import PartitionSpec as P
 
-GROUPS = ((128, False), (128, False), (128, False), (128, False))
+GROUPS = ((128, False), (128, False), (256, True))
 LEAF_LIMIT = 24 * 1024 * 1024
 LIMIT = 16 * 1024 * 1024
 
@@ -43,7 +43,8 @@
     return jnp.stack([real_part, imag_part])
 
 
-def leaf_kernel(start, width, apart, place, x_hbm, l_hbm, t_hbm, *refs):
+def leaf_kernel(start, width, apart, place, gates, x_hbm, l_hbm, t_hbm, *refs):
+    refs = refs[gates:]
     nodes = l_hbm.shape[0]
     outs, (x, l, t0, t1, sems) = refs[:-5], refs[-5:]
     if apart:
@@ -147,13 +148,13 @@
     def part(group, some):
         return jax.ShapeDtypeStruct((len(some), 2, rank, widths[group]), jnp.bfloat16)
 
-    def leaf(group):
+    def leaf(group, gates):
         width, apart = GROUPS[group]
         mine = [some for at, some in chunks if at == group]
         return pl.pallas_call(
-            functools.partial(leaf_kernel, starts[group], width, apart, places[1]),
+            functools.partial(leaf_kernel, starts[group], width, apart, places[1], len(gates)),
             out_shape=tuple(part(group, some) for some in mine) * 2,
-            in_specs=[anywhere] * 3,
+            in_specs=[anywhere] * 3 + [pl.BlockSpec(memory_space=pl.ANY)] * len(gates),
             out_specs=(here,) * (2 * len(mine)),
             scratch_shapes=[
                 pltpu.VMEM((nodes, 2, rows, width), jnp.bfloat16),
@@ -165,7 +166,7 @@
             compiler_params=params(LEAF_LIMIT),
             cost_estimate=cost,
             name="leaf",
-        )(*in_hbm)
+        )(*in_hbm, *gates)
 
     def own(level, chunk, held):
         group, some = chunk
@@ -215,10 +216,11 @@
             name="last",
         )(*operands)
 
-    held, flying = {}, {}
+    held, flying, gates = {}, {}, ()
     for group in range(len(GROUPS)):
         mine = [chunk for chunk in chunks if chunk[0] == group]
-        results = leaf(group)
+        results = leaf(group, gates)
+        gates = results[:1]
         for at, chunk in enumerate(mine):
             held[chunk] = results[at]
             flying[chunk] = partner_2(results[len(mine) + at], *places[1])

time: 114 us -> 114 us (level)
  waiting for transfers between devices: 60.7 us -> 63.2 us
  Pallas kernels: 24.6 us -> 22.8 us
    ppermute x12, waiting for transfers between devices: 60.7 us -> 63.2 us  [partner_2(): return lax.ppermute(block, axis, route)]
    pallas_call x4 -> x3, Pallas kernels: 15.3 us -> 13.3 us  [leaf(): pl.pallas_call(functools.partial(leaf_kernel, starts[group], width, apart...]
  transfers between devices with their start and end apart: 12 -> 12, of which waited for: 8 -> 8; matrix products, arithmetic and copies ran while one was open for 0% -> 0% of each run, Pallas kernels for 18% -> 16%
where the time goes in v5:
time: 114 us
  waiting for transfers between devices  63.2 us (55%)
  starting transfers between devices  27.4 us (24%)
  Pallas kernels  22.8 us (20%)
    ppermute x12, waiting for transfers between devices, partner_2(): return lax.ppermute(block, axis, route)  63.2 us
    ppermute x12, starting transfers between devices, partner_2(): return lax.ppermute(block, axis, route)  27.4 us
    pallas_call x3, Pallas kernels, leaf(): pl.pallas_call(functools.partial(leaf_kernel, starts[group], width, apart...  13.3 us
    pallas_call x8, Pallas kernels, middle(): pl.pallas_call(functools.partial(middle_kernel, level, some, places[level...  4.07 us
    pallas_call x4, Pallas kernels, last(): pl.pallas_call(functools.partial(last_kernel, level, some, starts[group],...  3 us
    pallas_call x8, Pallas kernels, own(): pl.pallas_call(functools.partial(own_kernel, level, some, places[level]),...  2.35 us
  transfers between devices with their start and end apart: 12, of which 8 were waited for; matrix products, arithmetic and copies ran while one was open for 0% of the time, Pallas kernels for 16%

profile of v5, /device:TPU:1, one launch (start us, length us, event | category | flops | bytes accessed | tf_op | source)
XLA Modules:
  0.0 113.8 jit_solution(16268317098835671751)
XLA Ops:
  0.0 3.8 %leaf.3 = (bf16[2,2,256,128]{3,2,1,0:T(8,128)(2,1)S(1)}, bf16[2,2,256,128]{3,2,1,0:T(8,128)(2,1)S(1)}) custom-call(bf16[2,2,1024,512]{3,2,1,0:T(8,128)(2,1)} %x_hbm.5, bf16[2,2,256,1024]{3,2,1,0:T(8,128)(2,1)} %l_hbm.5, bf16[4,2,2,2,256,256]{5,4,3,2,1,0:T(8,128)(2,1)} %t_ref.39), custom_call_target="tpu_custom_call" | custom-call | flops 2 | bytes 2 | tf_op jit(solution)/shard_map/leaf/pallas_call | solution.py:154
  3.8 7.8 %collective-permute-start.9 = (bf16[2,2,256,128]{3,2,1,0:T(8,128)(2,1)S(1)}, bf16[2,2,256,128]{3,2,1,0:T(8,128)(2,1)S(1)}, u32[]{:S(2)}, u32[]{:S(2)}) collective-permute-start(bf16[2,2,256,128]{3,2,1,0:T(8,128)(2,1)S(1)} %get-tuple-element.48), channel_id=1, source_target_pairs={{0,128},{128,0},{8,136},{136,8},{16,144},{144,16},{24,152},{152,24... | collective-permute-start | bytes 786440 | tf_op jit(solution)/shard_map/ppermute | solution.py:22
  11.7 3.8 %leaf.4 = (bf16[2,2,256,128]{3,2,1,0:T(8,128)(2,1)S(1)}, bf16[2,2,256,128]{3,2,1,0:T(8,128)(2,1)S(1)}) custom-call(bf16[2,2,1024,512]{3,2,1,0:T(8,128)(2,1)} %x_hbm.5, bf16[2,2,256,1024]{3,2,1,0:T(8,128)(2,1)} %l_hbm.5, bf16[4,2,2,2,256,256]{5,4,3,2,1,0:T(8,128)(2,1)} %t_ref.39, bf16[2,2,256,128]{3,2,1,0:T(8,128)(2,1)S(1)} %get-tuple-element.29.refs_0_.a_ref), custom_call_target="tpu_custom_call" | custom-call | flops 2 | bytes 2 | tf_op jit(solution)/shard_map/leaf/pallas_call | solution.py:154
  15.5 0.1 collective-permute-start.6
  15.6 5.7 %leaf.5 = (bf16[1,2,256,256]{3,2,1,0:T(8,128)(2,1)S(1)}, bf16[1,2,256,256]{3,2,1,0:T(8,128)(2,1)S(1)}, bf16[1,2,256,256]{3,2,1,0:T(8,128)(2,1)S(1)}, bf16[1,2,256,256]{3,2,1,0:T(8,128)(2,1)S(1)}) custom-call(bf16[2,2,1024,512]{3,2,1,0:T(8,128)(2,1)} %x_hbm.5, bf16[2,2,256,1024]{3,2,1,0:T(8,128)(2,1)} %l_hbm.5, bf16[4,2,2,2,256,256]{5,4,3,2,1,0:T(8,128)(2,1)} %t_ref.39, ...), custom_call_target="tpu_custom_call" | custom-call | flops 2 | bytes 2 | tf_op jit(solution)/shard_map/leaf/pallas_call | solution.py:154
  21.3 5.4 %collective-permute-start.3 = (bf16[1,2,256,256]{3,2,1,0:T(8,128)(2,1)S(1)}, bf16[1,2,256,256]{3,2,1,0:T(8,128)(2,1)S(1)}, u32[]{:S(2)}, u32[]{:S(2)}) collective-permute-start(bf16[1,2,256,256]{3,2,1,0:T(8,128)(2,1)S(1)} %get-tuple-element.38), channel_id=1, source_target_pairs={{0,128},{128,0},{8,136},{136,8},{16,144},{144,16},{24,152},{152,24... | collective-permute-start | bytes 786440 | tf_op jit(solution)/shard_map/ppermute | solution.py:22
  26.7 0.1 collective-permute-start
  26.8 0.0 collective-permute-done.9.in_ref
  26.8 0.0 copy-done
  26.8 0.7 middle.14
  27.5 1.4 %collective-permute-start.10 = (bf16[2,2,256,128]{3,2,1,0:T(8,128)(2,1)S(1)}, bf16[2,2,256,128]{3,2,1,0:T(8,128)(2,1)S(1)}, u32[]{:S(2)}, u32[]{:S(2)}) collective-permute-start(bf16[2,2,256,128]{3,2,1,0:T(8,128)(2,1)S(1)} %get-tuple-element.50), channel_id=1, source_target_pairs={{0,64},{64,0},{8,72},{72,8},{16,80},{80,16},{24,88},{88,24},{32,96... | collective-permute-start | bytes 786440 | tf_op jit(solution)/shard_map/ppermute | solution.py:22
  29.0 10.7 %collective-permute-done.6.in_ref = bf16[2,2,256,128]{3,2,1,0:T(8,128)(2,1)S(1)} collective-permute-done((bf16[2,2,256,128]{3,2,1,0:T(8,128)(2,1)S(1)}, bf16[2,2,256,128]{3,2,1,0:T(8,128)(2,1)S(1)}, u32[]{:S(2)}, u32[]{:S(2)}) %collective-permute-start.6) | collective-permute-done | bytes 262176 | tf_op jit(solution)/shard_map/ppermute | solution.py:22
  39.7 0.7 middle.12
  40.4 0.1 collective-permute-start.7
  40.5 14.3 %collective-permute-done.3.in_ref = bf16[1,2,256,256]{3,2,1,0:T(8,128)(2,1)S(1)} collective-permute-done((bf16[1,2,256,256]{3,2,1,0:T(8,128)(2,1)S(1)}, bf16[1,2,256,256]{3,2,1,0:T(8,128)(2,1)S(1)}, u32[]{:S(2)}, u32[]{:S(2)}) %collective-permute-start.3) | collective-permute-done | bytes 262176 | tf_op jit(solution)/shard_map/ppermute | solution.py:22
  54.7 0.7 middle.10
  55.5 0.1 collective-permute-start.4
  55.6 4.8 %collective-permute-done.in_ref = bf16[1,2,256,256]{3,2,1,0:T(8,128)(2,1)S(1)} collective-permute-done((bf16[1,2,256,256]{3,2,1,0:T(8,128)(2,1)S(1)}, bf16[1,2,256,256]{3,2,1,0:T(8,128)(2,1)S(1)}, u32[]{:S(2)}, u32[]{:S(2)}) %collective-permute-start) | collective-permute-done | bytes 262176 | tf_op jit(solution)/shard_map/ppermute | solution.py:22
  60.3 0.7 middle.8
  61.1 0.3 collective-permute-start.1
  61.4 0.3 own.14.a_ref
  61.7 0.3 own.12.a_ref
  62.0 0.3 own.10.a_ref
  62.3 0.3 own.8.a_ref
  62.6 24.1 %collective-permute-done.10.in_ref = bf16[2,2,256,128]{3,2,1,0:T(8,128)(2,1)S(1)} collective-permute-done((bf16[2,2,256,128]{3,2,1,0:T(8,128)(2,1)S(1)}, bf16[2,2,256,128]{3,2,1,0:T(8,128)(2,1)S(1)}, u32[]{:S(2)}, u32[]{:S(2)}) %collective-permute-start.10) | collective-permute-done | bytes 262176 | tf_op jit(solution)/shard_map/ppermute | solution.py:22
  86.7 0.3 middle.15
  87.0 3.0 %collective-permute-start.11 = (bf16[2,2,256,128]{3,2,1,0:T(8,128)(2,1)S(1)}, bf16[2,2,256,128]{3,2,1,0:T(8,128)(2,1)S(1)}, u32[]{:S(2)}, u32[]{:S(2)}) collective-permute-start(bf16[2,2,256,128]{3,2,1,0:T(8,128)(2,1)S(1)} %get-tuple-element.52), channel_id=1, source_target_pairs={{0,4},{4,0},{1,5},{5,1},{2,6},{6,2},{3,7},{7,3},{8,12},{12,8},{9,1... | collective-permute-start | bytes 786440 | tf_op jit(solution)/shard_map/ppermute | solution.py:22
  90.0 2.3 %collective-permute-done.7.in_ref = bf16[2,2,256,128]{3,2,1,0:T(8,128)(2,1)S(1)} collective-permute-done((bf16[2,2,256,128]{3,2,1,0:T(8,128)(2,1)S(1)}, bf16[2,2,256,128]{3,2,1,0:T(8,128)(2,1)S(1)}, u32[]{:S(2)}, u32[]{:S(2)}) %collective-permute-start.7) | collective-permute-done | bytes 262176 | tf_op jit(solution)/shard_map/ppermute | solution.py:22
  92.3 0.3 middle.13
  92.6 3.0 %collective-permute-start.8 = (bf16[2,2,256,128]{3,2,1,0:T(8,128)(2,1)S(1)}, bf16[2,2,256,128]{3,2,1,0:T(8,128)(2,1)S(1)}, u32[]{:S(2)}, u32[]{:S(2)}) collective-permute-start(bf16[2,2,256,128]{3,2,1,0:T(8,128)(2,1)S(1)} %get-tuple-element.47), channel_id=1, source_target_pairs={{0,4},{4,0},{1,5},{5,1},{2,6},{6,2},{3,7},{7,3},{8,12},{12,8},{9,1... | collective-permute-start | bytes 786440 | tf_op jit(solution)/shard_map/ppermute | solution.py:22
  95.6 2.3 %collective-permute-done.4.in_ref = bf16[1,2,256,256]{3,2,1,0:T(8,128)(2,1)S(1)} collective-permute-done((bf16[1,2,256,256]{3,2,1,0:T(8,128)(2,1)S(1)}, bf16[1,2,256,256]{3,2,1,0:T(8,128)(2,1)S(1)}, u32[]{:S(2)}, u32[]{:S(2)}) %collective-permute-start.4) | collective-permute-done | bytes 262176 | tf_op jit(solution)/shard_map/ppermute | solution.py:22
  97.9 0.3 middle.11
  98.2 3.0 %collective-permute-start.5 = (bf16[1,2,256,256]{3,2,1,0:T(8,128)(2,1)S(1)}, bf16[1,2,256,256]{3,2,1,0:T(8,128)(2,1)S(1)}, u32[]{:S(2)}, u32[]{:S(2)}) collective-permute-start(bf16[1,2,256,256]{3,2,1,0:T(8,128)(2,1)S(1)} %get-tuple-element.42), channel_id=1, source_target_pairs={{0,4},{4,0},{1,5},{5,1},{2,6},{6,2},{3,7},{7,3},{8,12},{12,8},{9,1... | collective-permute-start | bytes 786440 | tf_op jit(solution)/shard_map/ppermute | solution.py:22
  101.2 2.3 %collective-permute-done.1.in_ref = bf16[1,2,256,256]{3,2,1,0:T(8,128)(2,1)S(1)} collective-permute-done((bf16[1,2,256,256]{3,2,1,0:T(8,128)(2,1)S(1)}, bf16[1,2,256,256]{3,2,1,0:T(8,128)(2,1)S(1)}, u32[]{:S(2)}, u32[]{:S(2)}) %collective-permute-start.1) | collective-permute-done | bytes 262176 | tf_op jit(solution)/shard_map/ppermute | solution.py:22
  103.5 0.3 middle.9
  103.9 3.0 %collective-permute-start.2 = (bf16[1,2,256,256]{3,2,1,0:T(8,128)(2,1)S(1)}, bf16[1,2,256,256]{3,2,1,0:T(8,128)(2,1)S(1)}, u32[]{:S(2)}, u32[]{:S(2)}) collective-permute-start(bf16[1,2,256,256]{3,2,1,0:T(8,128)(2,1)S(1)} %get-tuple-element.36), channel_id=1, source_target_pairs={{0,4},{4,0},{1,5},{5,1},{2,6},{6,2},{3,7},{7,3},{8,12},{12,8},{9,1... | collective-permute-start | bytes 786440 | tf_op jit(solution)/shard_map/ppermute | solution.py:22
  106.9 0.3 own.15.a_ref
  107.2 0.3 own.13.a_ref
  107.5 0.3 own.11.a_ref
  107.8 0.3 own.9.a_ref
  108.1 0.0 collective-permute-done.11.in_ref
  108.1 0.7 last.4.refs_0_
  108.8 0.0 collective-permute-done.8.in_ref
  108.8 0.7 last.5.refs_0_
  109.6 0.0 collective-permute-done.5.in_ref
  109.6 0.8 last.6.refs_0_
  110.4 2.5 %collective-permute-done.2.in_ref = bf16[1,2,256,256]{3,2,1,0:T(8,128)(2,1)S(1)} collective-permute-done((bf16[1,2,256,256]{3,2,1,0:T(8,128)(2,1)S(1)}, bf16[1,2,256,256]{3,2,1,0:T(8,128)(2,1)S(1)}, u32[]{:S(2)}, u32[]{:S(2)}) %collective-permute-start.2) | collective-permute-done | bytes 262176 | tf_op jit(solution)/shard_map/ppermute | solution.py:22
  112.8 0.8 last.7
  (1 shorter events, 0.0 us)
Async XLA Ops:
  3.8 23.0 %collective-permute-start.9 = (bf16[2,2,256,128]{3,2,1,0:T(8,128)(2,1)S(1)}, bf16[2,2,256,128]{3,2,1,0:T(8,128)(2,1)S(1)}, u32[]{:S(2)}, u32[]{:S(2)}) collective-permute-start(bf16[2,2,256,128]{3,2,1,0:T(8,128)(2,1)S(1)} %get-tuple-element.48), channel_id=1, source_target_pairs={{0,128},{128,0},{8,136},{136,8},{16,144},{144,16},{24,152},{152,24... | collective-permute-start | bytes 786440 | tf_op jit(solution)/shard_map/ppermute | solution.py:22
  15.5 24.2 %collective-permute-start.6 = (bf16[2,2,256,128]{3,2,1,0:T(8,128)(2,1)S(1)}, bf16[2,2,256,128]{3,2,1,0:T(8,128)(2,1)S(1)}, u32[]{:S(2)}, u32[]{:S(2)}) collective-permute-start(bf16[2,2,256,128]{3,2,1,0:T(8,128)(2,1)S(1)} %get-tuple-element.43), channel_id=1, source_target_pairs={{0,128},{128,0},{8,136},{136,8},{16,144},{144,16},{24,152},{152,24... | collective-permute-start | bytes 786440 | tf_op jit(solution)/shard_map/ppermute | solution.py:22
  15.6 11.2 %copy-start = (bf16[4,2,2,2,256,256]{5,4,3,2,1,0:T(8,128)(2,1)S(1)}, bf16[4,2,2,2,256,256]{5,4,3,2,1,0:T(8,128)(2,1)}, u32[]{:S(2)}) copy-start(bf16[4,2,2,2,256,256]{5,4,3,2,1,0:T(8,128)(2,1)} %t_ref.39) | copy-start | bytes 12582916
  21.3 33.4 %collective-permute-start.3 = (bf16[1,2,256,256]{3,2,1,0:T(8,128)(2,1)S(1)}, bf16[1,2,256,256]{3,2,1,0:T(8,128)(2,1)S(1)}, u32[]{:S(2)}, u32[]{:S(2)}) collective-permute-start(bf16[1,2,256,256]{3,2,1,0:T(8,128)(2,1)S(1)} %get-tuple-element.38), channel_id=1, source_target_pairs={{0,128},{128,0},{8,136},{136,8},{16,144},{144,16},{24,152},{152,24... | collective-permute-start | bytes 786440 | tf_op jit(solution)/shard_map/ppermute | solution.py:22
  26.7 33.6 %collective-permute-start = (bf16[1,2,256,256]{3,2,1,0:T(8,128)(2,1)S(1)}, bf16[1,2,256,256]{3,2,1,0:T(8,128)(2,1)S(1)}, u32[]{:S(2)}, u32[]{:S(2)}) collective-permute-start(bf16[1,2,256,256]{3,2,1,0:T(8,128)(2,1)S(1)} %get-tuple-element.32), channel_id=1, source_target_pairs={{0,128},{128,0},{8,136},{136,8},{16,144},{144,16},{24,152},{152,24... | collective-permute-start | bytes 786440 | tf_op jit(solution)/shard_map/ppermute | solution.py:22
  27.5 59.2 %collective-permute-start.10 = (bf16[2,2,256,128]{3,2,1,0:T(8,128)(2,1)S(1)}, bf16[2,2,256,128]{3,2,1,0:T(8,128)(2,1)S(1)}, u32[]{:S(2)}, u32[]{:S(2)}) collective-permute-start(bf16[2,2,256,128]{3,2,1,0:T(8,128)(2,1)S(1)} %get-tuple-element.50), channel_id=1, source_target_pairs={{0,64},{64,0},{8,72},{72,8},{16,80},{80,16},{24,88},{88,24},{32,96... | collective-permute-start | bytes 786440 | tf_op jit(solution)/shard_map/ppermute | solution.py:22
  40.4 51.9 %collective-permute-start.7 = (bf16[2,2,256,128]{3,2,1,0:T(8,128)(2,1)S(1)}, bf16[2,2,256,128]{3,2,1,0:T(8,128)(2,1)S(1)}, u32[]{:S(2)}, u32[]{:S(2)}) collective-permute-start(bf16[2,2,256,128]{3,2,1,0:T(8,128)(2,1)S(1)} %get-tuple-element.45), channel_id=1, source_target_pairs={{0,64},{64,0},{8,72},{72,8},{16,80},{80,16},{24,88},{88,24},{32,96... | collective-permute-start | bytes 786440 | tf_op jit(solution)/shard_map/ppermute | solution.py:22
  55.5 42.5 %collective-permute-start.4 = (bf16[1,2,256,256]{3,2,1,0:T(8,128)(2,1)S(1)}, bf16[1,2,256,256]{3,2,1,0:T(8,128)(2,1)S(1)}, u32[]{:S(2)}, u32[]{:S(2)}) collective-permute-start(bf16[1,2,256,256]{3,2,1,0:T(8,128)(2,1)S(1)} %get-tuple-element.40), channel_id=1, source_target_pairs={{0,64},{64,0},{8,72},{72,8},{16,80},{80,16},{24,88},{88,24},{32,96... | collective-permute-start | bytes 786440 | tf_op jit(solution)/shard_map/ppermute | solution.py:22
  61.1 42.5 %collective-permute-start.1 = (bf16[1,2,256,256]{3,2,1,0:T(8,128)(2,1)S(1)}, bf16[1,2,256,256]{3,2,1,0:T(8,128)(2,1)S(1)}, u32[]{:S(2)}, u32[]{:S(2)}) collective-permute-start(bf16[1,2,256,256]{3,2,1,0:T(8,128)(2,1)S(1)} %get-tuple-element.34), channel_id=1, source_target_pairs={{0,64},{64,0},{8,72},{72,8},{16,80},{80,16},{24,88},{88,24},{32,96... | collective-permute-start | bytes 786440 | tf_op jit(solution)/shard_map/ppermute | solution.py:22
  87.0 21.1 %collective-permute-start.11 = (bf16[2,2,256,128]{3,2,1,0:T(8,128)(2,1)S(1)}, bf16[2,2,256,128]{3,2,1,0:T(8,128)(2,1)S(1)}, u32[]{:S(2)}, u32[]{:S(2)}) collective-permute-start(bf16[2,2,256,128]{3,2,1,0:T(8,128)(2,1)S(1)} %get-tuple-element.52), channel_id=1, source_target_pairs={{0,4},{4,0},{1,5},{5,1},{2,6},{6,2},{3,7},{7,3},{8,12},{12,8},{9,1... | collective-permute-start | bytes 786440 | tf_op jit(solution)/shard_map/ppermute | solution.py:22
  92.6 16.2 %collective-permute-start.8 = (bf16[2,2,256,128]{3,2,1,0:T(8,128)(2,1)S(1)}, bf16[2,2,256,128]{3,2,1,0:T(8,128)(2,1)S(1)}, u32[]{:S(2)}, u32[]{:S(2)}) collective-permute-start(bf16[2,2,256,128]{3,2,1,0:T(8,128)(2,1)S(1)} %get-tuple-element.47), channel_id=1, source_target_pairs={{0,4},{4,0},{1,5},{5,1},{2,6},{6,2},{3,7},{7,3},{8,12},{12,8},{9,1... | collective-permute-start | bytes 786440 | tf_op jit(solution)/shard_map/ppermute | solution.py:22
  98.2 11.4 %collective-permute-start.5 = (bf16[1,2,256,256]{3,2,1,0:T(8,128)(2,1)S(1)}, bf16[1,2,256,256]{3,2,1,0:T(8,128)(2,1)S(1)}, u32[]{:S(2)}, u32[]{:S(2)}) collective-permute-start(bf16[1,2,256,256]{3,2,1,0:T(8,128)(2,1)S(1)} %get-tuple-element.42), channel_id=1, source_target_pairs={{0,4},{4,0},{1,5},{5,1},{2,6},{6,2},{3,7},{7,3},{8,12},{12,8},{9,1... | collective-permute-start | bytes 786440 | tf_op jit(solution)/shard_map/ppermute | solution.py:22
  103.9 9.0 %collective-permute-start.2 = (bf16[1,2,256,256]{3,2,1,0:T(8,128)(2,1)S(1)}, bf16[1,2,256,256]{3,2,1,0:T(8,128)(2,1)S(1)}, u32[]{:S(2)}, u32[]{:S(2)}) collective-permute-start(bf16[1,2,256,256]{3,2,1,0:T(8,128)(2,1)S(1)} %get-tuple-element.36), channel_id=1, source_target_pairs={{0,4},{4,0},{1,5},{5,1},{2,6},{6,2},{3,7},{7,3},{8,12},{12,8},{9,1... | collective-permute-start | bytes 786440 | tf_op jit(solution)/shard_map/ppermute | solution.py:22

commit v6 on v4

--- a/solution.py
+++ b/solution.py
@@ -220,8 +220,8 @@
         mine = [chunk for chunk in chunks if chunk[0] == group]
         results = leaf(group)
         for at, chunk in enumerate(mine):
-            held[chunk] = results[at]
             flying[chunk] = partner_2(results[len(mine) + at], *places[1])
+            held[chunk] = own(1, chunk, results[at])
     for level in (1, 2):
         for chunk in chunks:
             held[chunk], term = middle(level, chunk, held[chunk], flying[chunk])

time: 114 us -> 114 us (level)
    pallas_call x8, Pallas kernels: 3.91 us -> 2.46 us  [middle(): pl.pallas_call(functools.partial(middle_kernel, level, some, places[level...]
    pallas_call x8 -> x12, Pallas kernels: 2.36 us -> 3.54 us  [own(): pl.pallas_call(functools.partial(own_kernel, level, some, places[level]),...]
  transfers between devices with their start and end apart: 12 -> 12, of which waited for: 8 -> 8; matrix products, arithmetic and copies ran while one was open for 0% -> 0% of each run, Pallas kernels for 18% -> 17%
where the time goes in v6:
time: 114 us
  waiting for transfers between devices  61.3 us (54%)
  starting transfers between devices  27.6 us (24%)
  Pallas kernels  24.3 us (21%)
    ppermute x12, waiting for transfers between devices, partner_2(): return lax.ppermute(block, axis, route)  61.3 us
    ppermute x12, starting transfers between devices, partner_2(): return lax.ppermute(block, axis, route)  27.6 us
    pallas_call x4, Pallas kernels, leaf(): pl.pallas_call(functools.partial(leaf_kernel, starts[group], width, apart...  15.3 us
    pallas_call x12, Pallas kernels, own(): pl.pallas_call(functools.partial(own_kernel, level, some, places[level]),...  3.54 us
    pallas_call x4, Pallas kernels, last(): pl.pallas_call(functools.partial(last_kernel, level, some, starts[group],...  2.97 us
    pallas_call x8, Pallas kernels, middle(): pl.pallas_call(functools.partial(middle_kernel, level, some, places[level...  2.46 us
  transfers between devices with their start and end apart: 12, of which 8 were waited for; matrix products, arithmetic and copies ran while one was open for 0% of the time, Pallas kernels for 17%

profile of v6, /device:TPU:1, one launch (start us, length us, event | category | flops | bytes accessed | tf_op | source)
XLA Modules:
  0.0 113.6 jit_solution(3377596368787999452)
XLA Ops:
  0.0 3.8 %leaf.7 = (bf16[2,2,256,128]{3,2,1,0:T(8,128)(2,1)S(1)}, bf16[2,2,256,128]{3,2,1,0:T(8,128)(2,1)S(1)}) custom-call(bf16[2,2,1024,512]{3,2,1,0:T(8,128)(2,1)} %x_hbm.7, bf16[2,2,256,1024]{3,2,1,0:T(8,128)(2,1)} %l_hbm.7, bf16[4,2,2,2,256,256]{5,4,3,2,1,0:T(8,128)(2,1)} %t_ref.47), custom_call_target="tpu_custom_call" | custom-call | flops 2 | bytes 2 | tf_op jit(solution)/shard_map/leaf/pallas_call | solution.py:153
  3.8 7.8 %collective-permute-start.9 = (bf16[2,2,256,128]{3,2,1,0:T(8,128)(2,1)S(1)}, bf16[2,2,256,128]{3,2,1,0:T(8,128)(2,1)S(1)}, u32[]{:S(2)}, u32[]{:S(2)}) collective-permute-start(bf16[2,2,256,128]{3,2,1,0:T(8,128)(2,1)S(1)} %get-tuple-element.48), channel_id=1, source_target_pairs={{0,128},{128,0},{8,136},{136,8},{16,144},{144,16},{24,152},{152,24... | collective-permute-start | bytes 786440 | tf_op jit(solution)/shard_map/ppermute | solution.py:22
  11.7 3.8 %leaf.6 = (bf16[2,2,256,128]{3,2,1,0:T(8,128)(2,1)S(1)}, bf16[2,2,256,128]{3,2,1,0:T(8,128)(2,1)S(1)}) custom-call(bf16[2,2,1024,512]{3,2,1,0:T(8,128)(2,1)} %x_hbm.7, bf16[2,2,256,1024]{3,2,1,0:T(8,128)(2,1)} %l_hbm.7, bf16[4,2,2,2,256,256]{5,4,3,2,1,0:T(8,128)(2,1)} %t_ref.47), custom_call_target="tpu_custom_call" | custom-call | flops 2 | bytes 2 | tf_op jit(solution)/shard_map/leaf/pallas_call | solution.py:153
  15.5 0.1 collective-permute-start.6
  15.6 3.8 %leaf.5 = (bf16[2,2,256,128]{3,2,1,0:T(8,128)(2,1)S(1)}, bf16[2,2,256,128]{3,2,1,0:T(8,128)(2,1)S(1)}) custom-call(bf16[2,2,1024,512]{3,2,1,0:T(8,128)(2,1)} %x_hbm.7, bf16[2,2,256,1024]{3,2,1,0:T(8,128)(2,1)} %l_hbm.7, bf16[4,2,2,2,256,256]{5,4,3,2,1,0:T(8,128)(2,1)} %t_ref.47), custom_call_target="tpu_custom_call" | custom-call | flops 2 | bytes 2 | tf_op jit(solution)/shard_map/leaf/pallas_call | solution.py:153
  19.5 5.4 %collective-permute-start.3 = (bf16[2,2,256,128]{3,2,1,0:T(8,128)(2,1)S(1)}, bf16[2,2,256,128]{3,2,1,0:T(8,128)(2,1)S(1)}, u32[]{:S(2)}, u32[]{:S(2)}) collective-permute-start(bf16[2,2,256,128]{3,2,1,0:T(8,128)(2,1)S(1)} %get-tuple-element.36), channel_id=1, source_target_pairs={{0,128},{128,0},{8,136},{136,8},{16,144},{144,16},{24,152},{152,24... | collective-permute-start | bytes 786440 | tf_op jit(solution)/shard_map/ppermute | solution.py:22
  24.9 3.8 %leaf.4 = (bf16[2,2,256,128]{3,2,1,0:T(8,128)(2,1)S(1)}, bf16[2,2,256,128]{3,2,1,0:T(8,128)(2,1)S(1)}) custom-call(bf16[2,2,1024,512]{3,2,1,0:T(8,128)(2,1)} %x_hbm.7, bf16[2,2,256,1024]{3,2,1,0:T(8,128)(2,1)} %l_hbm.7, bf16[4,2,2,2,256,256]{5,4,3,2,1,0:T(8,128)(2,1)} %t_ref.47), custom_call_target="tpu_custom_call" | custom-call | flops 2 | bytes 2 | tf_op jit(solution)/shard_map/leaf/pallas_call | solution.py:153
  28.7 0.2 collective-permute-start
  29.0 0.3 own.21.a_ref
  29.3 0.3 own.18.a_ref
  29.6 0.3 own.15.a_ref
  29.9 0.3 own.12.a_ref
  30.2 0.3 middle.14
  30.5 1.6 %collective-permute-start.10 = (bf16[2,2,256,128]{3,2,1,0:T(8,128)(2,1)S(1)}, bf16[2,2,256,128]{3,2,1,0:T(8,128)(2,1)S(1)}, u32[]{:S(2)}, u32[]{:S(2)}) collective-permute-start(bf16[2,2,256,128]{3,2,1,0:T(8,128)(2,1)S(1)} %get-tuple-element.50), channel_id=1, source_target_pairs={{0,64},{64,0},{8,72},{72,8},{16,80},{80,16},{24,88},{88,24},{32,96... | collective-permute-start | bytes 786440 | tf_op jit(solution)/shard_map/ppermute | solution.py:22
  32.1 7.5 %collective-permute-done.6.in_ref = bf16[2,2,256,128]{3,2,1,0:T(8,128)(2,1)S(1)} collective-permute-done((bf16[2,2,256,128]{3,2,1,0:T(8,128)(2,1)S(1)}, bf16[2,2,256,128]{3,2,1,0:T(8,128)(2,1)S(1)}, u32[]{:S(2)}, u32[]{:S(2)}) %collective-permute-start.6) | collective-permute-done | bytes 262176 | tf_op jit(solution)/shard_map/ppermute | solution.py:22
  39.6 0.3 middle.12
  39.9 0.1 collective-permute-start.7
  40.0 14.7 %collective-permute-done.3.in_ref = bf16[2,2,256,128]{3,2,1,0:T(8,128)(2,1)S(1)} collective-permute-done((bf16[2,2,256,128]{3,2,1,0:T(8,128)(2,1)S(1)}, bf16[2,2,256,128]{3,2,1,0:T(8,128)(2,1)S(1)}, u32[]{:S(2)}, u32[]{:S(2)}) %collective-permute-start.3) | collective-permute-done | bytes 262176 | tf_op jit(solution)/shard_map/ppermute | solution.py:22
  54.7 0.3 middle.10
  55.0 0.1 collective-permute-start.4
  55.1 5.2 %collective-permute-done.in_ref = bf16[2,2,256,128]{3,2,1,0:T(8,128)(2,1)S(1)} collective-permute-done((bf16[2,2,256,128]{3,2,1,0:T(8,128)(2,1)S(1)}, bf16[2,2,256,128]{3,2,1,0:T(8,128)(2,1)S(1)}, u32[]{:S(2)}, u32[]{:S(2)}) %collective-permute-start) | collective-permute-done | bytes 262176 | tf_op jit(solution)/shard_map/ppermute | solution.py:22
  60.3 0.3 middle.8
  60.6 0.3 collective-permute-start.1
  60.9 0.3 own.22.a_ref
  61.2 0.3 own.19.a_ref
  61.5 0.3 own.16.a_ref
  61.8 0.3 own.13.a_ref
  62.1 24.5 %collective-permute-done.10.in_ref = bf16[2,2,256,128]{3,2,1,0:T(8,128)(2,1)S(1)} collective-permute-done((bf16[2,2,256,128]{3,2,1,0:T(8,128)(2,1)S(1)}, bf16[2,2,256,128]{3,2,1,0:T(8,128)(2,1)S(1)}, u32[]{:S(2)}, u32[]{:S(2)}) %collective-permute-start.10) | collective-permute-done | bytes 262176 | tf_op jit(solution)/shard_map/ppermute | solution.py:22
  86.6 0.3 middle.15
  86.9 3.0 %collective-permute-start.11 = (bf16[2,2,256,128]{3,2,1,0:T(8,128)(2,1)S(1)}, bf16[2,2,256,128]{3,2,1,0:T(8,128)(2,1)S(1)}, u32[]{:S(2)}, u32[]{:S(2)}) collective-permute-start(bf16[2,2,256,128]{3,2,1,0:T(8,128)(2,1)S(1)} %get-tuple-element.52), channel_id=1, source_target_pairs={{0,4},{4,0},{1,5},{5,1},{2,6},{6,2},{3,7},{7,3},{8,12},{12,8},{9,1... | collective-permute-start | bytes 786440 | tf_op jit(solution)/shard_map/ppermute | solution.py:22
  89.9 2.3 %collective-permute-done.7.in_ref = bf16[2,2,256,128]{3,2,1,0:T(8,128)(2,1)S(1)} collective-permute-done((bf16[2,2,256,128]{3,2,1,0:T(8,128)(2,1)S(1)}, bf16[2,2,256,128]{3,2,1,0:T(8,128)(2,1)S(1)}, u32[]{:S(2)}, u32[]{:S(2)}) %collective-permute-start.7) | collective-permute-done | bytes 262176 | tf_op jit(solution)/shard_map/ppermute | solution.py:22
  92.2 0.3 middle.13
  92.5 3.0 %collective-permute-start.8 = (bf16[2,2,256,128]{3,2,1,0:T(8,128)(2,1)S(1)}, bf16[2,2,256,128]{3,2,1,0:T(8,128)(2,1)S(1)}, u32[]{:S(2)}, u32[]{:S(2)}) collective-permute-start(bf16[2,2,256,128]{3,2,1,0:T(8,128)(2,1)S(1)} %get-tuple-element.46), channel_id=1, source_target_pairs={{0,4},{4,0},{1,5},{5,1},{2,6},{6,2},{3,7},{7,3},{8,12},{12,8},{9,1... | collective-permute-start | bytes 786440 | tf_op jit(solution)/shard_map/ppermute | solution.py:22
  95.5 2.3 %collective-permute-done.4.in_ref = bf16[2,2,256,128]{3,2,1,0:T(8,128)(2,1)S(1)} collective-permute-done((bf16[2,2,256,128]{3,2,1,0:T(8,128)(2,1)S(1)}, bf16[2,2,256,128]{3,2,1,0:T(8,128)(2,1)S(1)}, u32[]{:S(2)}, u32[]{:S(2)}) %collective-permute-start.4) | collective-permute-done | bytes 262176 | tf_op jit(solution)/shard_map/ppermute | solution.py:22
  97.8 0.3 middle.11
  98.1 3.0 %collective-permute-start.5 = (bf16[2,2,256,128]{3,2,1,0:T(8,128)(2,1)S(1)}, bf16[2,2,256,128]{3,2,1,0:T(8,128)(2,1)S(1)}, u32[]{:S(2)}, u32[]{:S(2)}) collective-permute-start(bf16[2,2,256,128]{3,2,1,0:T(8,128)(2,1)S(1)} %get-tuple-element.40), channel_id=1, source_target_pairs={{0,4},{4,0},{1,5},{5,1},{2,6},{6,2},{3,7},{7,3},{8,12},{12,8},{9,1... | collective-permute-start | bytes 786440 | tf_op jit(solution)/shard_map/ppermute | solution.py:22
  101.1 2.3 %collective-permute-done.1.in_ref = bf16[2,2,256,128]{3,2,1,0:T(8,128)(2,1)S(1)} collective-permute-done((bf16[2,2,256,128]{3,2,1,0:T(8,128)(2,1)S(1)}, bf16[2,2,256,128]{3,2,1,0:T(8,128)(2,1)S(1)}, u32[]{:S(2)}, u32[]{:S(2)}) %collective-permute-start.1) | collective-permute-done | bytes 262176 | tf_op jit(solution)/shard_map/ppermute | solution.py:22
  103.4 0.3 middle.9
  103.8 3.0 %collective-permute-start.2 = (bf16[2,2,256,128]{3,2,1,0:T(8,128)(2,1)S(1)}, bf16[2,2,256,128]{3,2,1,0:T(8,128)(2,1)S(1)}, u32[]{:S(2)}, u32[]{:S(2)}) collective-permute-start(bf16[2,2,256,128]{3,2,1,0:T(8,128)(2,1)S(1)} %get-tuple-element.34), channel_id=1, source_target_pairs={{0,4},{4,0},{1,5},{5,1},{2,6},{6,2},{3,7},{7,3},{8,12},{12,8},{9,1... | collective-permute-start | bytes 786440 | tf_op jit(solution)/shard_map/ppermute | solution.py:22
  106.8 0.3 own.23.a_ref
  107.0 0.3 own.20.a_ref
  107.4 0.3 own.17.a_ref
  107.7 0.3 own.14.a_ref
  108.0 0.7 last.4.refs_0_
  108.7 0.7 last.5.refs_0_
  109.5 0.7 last.6.refs_0_
  110.2 2.5 %collective-permute-done.2.in_ref = bf16[2,2,256,128]{3,2,1,0:T(8,128)(2,1)S(1)} collective-permute-done((bf16[2,2,256,128]{3,2,1,0:T(8,128)(2,1)S(1)}, bf16[2,2,256,128]{3,2,1,0:T(8,128)(2,1)S(1)}, u32[]{:S(2)}, u32[]{:S(2)}) %collective-permute-start.2) | collective-permute-done | bytes 262176 | tf_op jit(solution)/shard_map/ppermute | solution.py:22
  112.7 0.7 last.7
  (6 shorter events, 0.0 us)
Async XLA Ops:
  3.8 26.4 %collective-permute-start.9 = (bf16[2,2,256,128]{3,2,1,0:T(8,128)(2,1)S(1)}, bf16[2,2,256,128]{3,2,1,0:T(8,128)(2,1)S(1)}, u32[]{:S(2)}, u32[]{:S(2)}) collective-permute-start(bf16[2,2,256,128]{3,2,1,0:T(8,128)(2,1)S(1)} %get-tuple-element.48), channel_id=1, source_target_pairs={{0,128},{128,0},{8,136},{136,8},{16,144},{144,16},{24,152},{152,24... | collective-permute-start | bytes 786440 | tf_op jit(solution)/shard_map/ppermute | solution.py:22
  15.5 24.1 %collective-permute-start.6 = (bf16[2,2,256,128]{3,2,1,0:T(8,128)(2,1)S(1)}, bf16[2,2,256,128]{3,2,1,0:T(8,128)(2,1)S(1)}, u32[]{:S(2)}, u32[]{:S(2)}) collective-permute-start(bf16[2,2,256,128]{3,2,1,0:T(8,128)(2,1)S(1)} %get-tuple-element.42), channel_id=1, source_target_pairs={{0,128},{128,0},{8,136},{136,8},{16,144},{144,16},{24,152},{152,24... | collective-permute-start | bytes 786440 | tf_op jit(solution)/shard_map/ppermute | solution.py:22
  19.5 9.5 %copy-start = (bf16[4,2,2,2,256,256]{5,4,3,2,1,0:T(8,128)(2,1)S(1)}, bf16[4,2,2,2,256,256]{5,4,3,2,1,0:T(8,128)(2,1)}, u32[]{:S(2)}) copy-start(bf16[4,2,2,2,256,256]{5,4,3,2,1,0:T(8,128)(2,1)} %t_ref.47) | copy-start | bytes 12582916
  19.5 35.2 %collective-permute-start.3 = (bf16[2,2,256,128]{3,2,1,0:T(8,128)(2,1)S(1)}, bf16[2,2,256,128]{3,2,1,0:T(8,128)(2,1)S(1)}, u32[]{:S(2)}, u32[]{:S(2)}) collective-permute-start(bf16[2,2,256,128]{3,2,1,0:T(8,128)(2,1)S(1)} %get-tuple-element.36), channel_id=1, source_target_pairs={{0,128},{128,0},{8,136},{136,8},{16,144},{144,16},{24,152},{152,24... | collective-permute-start | bytes 786440 | tf_op jit(solution)/shard_map/ppermute | solution.py:22
  28.7 31.6 %collective-permute-start = (bf16[2,2,256,128]{3,2,1,0:T(8,128)(2,1)S(1)}, bf16[2,2,256,128]{3,2,1,0:T(8,128)(2,1)S(1)}, u32[]{:S(2)}, u32[]{:S(2)}) collective-permute-start(bf16[2,2,256,128]{3,2,1,0:T(8,128)(2,1)S(1)} %get-tuple-element.30), channel_id=1, source_target_pairs={{0,128},{128,0},{8,136},{136,8},{16,144},{144,16},{24,152},{152,24... | collective-permute-start | bytes 786440 | tf_op jit(solution)/shard_map/ppermute | solution.py:22
  30.5 56.1 %collective-permute-start.10 = (bf16[2,2,256,128]{3,2,1,0:T(8,128)(2,1)S(1)}, bf16[2,2,256,128]{3,2,1,0:T(8,128)(2,1)S(1)}, u32[]{:S(2)}, u32[]{:S(2)}) collective-permute-start(bf16[2,2,256,128]{3,2,1,0:T(8,128)(2,1)S(1)} %get-tuple-element.50), channel_id=1, source_target_pairs={{0,64},{64,0},{8,72},{72,8},{16,80},{80,16},{24,88},{88,24},{32,96... | collective-permute-start | bytes 786440 | tf_op jit(solution)/shard_map/ppermute | solution.py:22
  39.9 52.3 %collective-permute-start.7 = (bf16[2,2,256,128]{3,2,1,0:T(8,128)(2,1)S(1)}, bf16[2,2,256,128]{3,2,1,0:T(8,128)(2,1)S(1)}, u32[]{:S(2)}, u32[]{:S(2)}) collective-permute-start(bf16[2,2,256,128]{3,2,1,0:T(8,128)(2,1)S(1)} %get-tuple-element.44), channel_id=1, source_target_pairs={{0,64},{64,0},{8,72},{72,8},{16,80},{80,16},{24,88},{88,24},{32,96... | collective-permute-start | bytes 786440 | tf_op jit(solution)/shard_map/ppermute | solution.py:22
  55.0 42.8 %collective-permute-start.4 = (bf16[2,2,256,128]{3,2,1,0:T(8,128)(2,1)S(1)}, bf16[2,2,256,128]{3,2,1,0:T(8,128)(2,1)S(1)}, u32[]{:S(2)}, u32[]{:S(2)}) collective-permute-start(bf16[2,2,256,128]{3,2,1,0:T(8,128)(2,1)S(1)} %get-tuple-element.38), channel_id=1, source_target_pairs={{0,64},{64,0},{8,72},{72,8},{16,80},{80,16},{24,88},{88,24},{32,96... | collective-permute-start | bytes 786440 | tf_op jit(solution)/shard_map/ppermute | solution.py:22
  60.6 42.8 %collective-permute-start.1 = (bf16[2,2,256,128]{3,2,1,0:T(8,128)(2,1)S(1)}, bf16[2,2,256,128]{3,2,1,0:T(8,128)(2,1)S(1)}, u32[]{:S(2)}, u32[]{:S(2)}) collective-permute-start(bf16[2,2,256,128]{3,2,1,0:T(8,128)(2,1)S(1)} %get-tuple-element.32), channel_id=1, source_target_pairs={{0,64},{64,0},{8,72},{72,8},{16,80},{80,16},{24,88},{88,24},{32,96... | collective-permute-start | bytes 786440 | tf_op jit(solution)/shard_map/ppermute | solution.py:22
  86.9 21.1 %collective-permute-start.11 = (bf16[2,2,256,128]{3,2,1,0:T(8,128)(2,1)S(1)}, bf16[2,2,256,128]{3,2,1,0:T(8,128)(2,1)S(1)}, u32[]{:S(2)}, u32[]{:S(2)}) collective-permute-start(bf16[2,2,256,128]{3,2,1,0:T(8,128)(2,1)S(1)} %get-tuple-element.52), channel_id=1, source_target_pairs={{0,4},{4,0},{1,5},{5,1},{2,6},{6,2},{3,7},{7,3},{8,12},{12,8},{9,1... | collective-permute-start | bytes 786440 | tf_op jit(solution)/shard_map/ppermute | solution.py:22
  92.5 16.2 %collective-permute-start.8 = (bf16[2,2,256,128]{3,2,1,0:T(8,128)(2,1)S(1)}, bf16[2,2,256,128]{3,2,1,0:T(8,128)(2,1)S(1)}, u32[]{:S(2)}, u32[]{:S(2)}) collective-permute-start(bf16[2,2,256,128]{3,2,1,0:T(8,128)(2,1)S(1)} %get-tuple-element.46), channel_id=1, source_target_pairs={{0,4},{4,0},{1,5},{5,1},{2,6},{6,2},{3,7},{7,3},{8,12},{12,8},{9,1... | collective-permute-start | bytes 786440 | tf_op jit(solution)/shard_map/ppermute | solution.py:22
  98.1 11.3 %collective-permute-start.5 = (bf16[2,2,256,128]{3,2,1,0:T(8,128)(2,1)S(1)}, bf16[2,2,256,128]{3,2,1,0:T(8,128)(2,1)S(1)}, u32[]{:S(2)}, u32[]{:S(2)}) collective-permute-start(bf16[2,2,256,128]{3,2,1,0:T(8,128)(2,1)S(1)} %get-tuple-element.40), channel_id=1, source_target_pairs={{0,4},{4,0},{1,5},{5,1},{2,6},{6,2},{3,7},{7,3},{8,12},{12,8},{9,1... | collective-permute-start | bytes 786440 | tf_op jit(solution)/shard_map/ppermute | solution.py:22
  103.8 9.0 %collective-permute-start.2 = (bf16[2,2,256,128]{3,2,1,0:T(8,128)(2,1)S(1)}, bf16[2,2,256,128]{3,2,1,0:T(8,128)(2,1)S(1)}, u32[]{:S(2)}, u32[]{:S(2)}) collective-permute-start(bf16[2,2,256,128]{3,2,1,0:T(8,128)(2,1)S(1)} %get-tuple-element.34), channel_id=1, source_target_pairs={{0,4},{4,0},{1,5},{5,1},{2,6},{6,2},{3,7},{7,3},{8,12},{12,8},{9,1... | collective-permute-start | bytes 786440 | tf_op jit(solution)/shard_map/ppermute | solution.py:22
